TPU v7x, 32 devices: a whole 2x2x4 slice. The times are simulated.
32 devices in a mesh: seq: 32 (over z, y, x, core).
Axes of the slice: x: 2, y: 2, z: 4, core: 2. Of those that a mesh axis runs over, the one named last changes fastest.
Arguments:
- incoming_hidden: bfloat16 [2, 16384, 768], P(None, 'seq'), may hold values from -6 to 6
- packed_run_lengths: int32 [2, 8], replicated, may hold values from 1 to 8192, 16384 in all within a row
- prior_standardize_factor: float32 [768], replicated, may hold values from 0.5 to 1.5
- prior_standardize_addend: float32 [768], replicated, may hold values from -3 to 3
- respond_interpolant: float32 [768], replicated, may hold values from 0 to 1
- address_interpolant: float32 [768], replicated, may hold values from 0 to 1
- content_interpolant: float32 [768], replicated, may hold values from 0 to 1
- valve_interpolant: float32 [768], replicated, may hold values from 0 to 1
- respond_transform: bfloat16 [768, 768], replicated, may hold values from -0.21875 to 0.21875
- address_transform: bfloat16 [768, 768], replicated, may hold values from -0.21875 to 0.21875
- content_transform: bfloat16 [768, 768], replicated, may hold values from -0.21875 to 0.21875
- valve_transform: bfloat16 [768, 768], replicated, may hold values from -0.21875 to 0.21875
- damping_rates: float32 [768], replicated, may hold values from -12 to -3.4
- immediate_boost: float32 [768], replicated, may hold values from -3 to 3
- cluster_normal_factor: float32 [768], replicated, may hold values from 0.5 to 1.5
- cluster_normal_shift_term: float32 [768], replicated, may hold values from -3 to 3
- readout_transform: bfloat16 [768, 768], replicated, may hold values from -0.4375 to 0.4375
- posterior_standardize_factor: float32 [768], replicated, may hold values from 0.5 to 1.5
- posterior_standardize_addend: float32 [768], replicated, may hold values from -3 to 3
- dense_address_interpolant: float32 [768], replicated, may hold values from 0 to 1
- dense_respond_interpolant: float32 [768], replicated, may hold values from 0 to 1
- dense_address_transform: bfloat16 [768, 2688], replicated, may hold values from -0.21875 to 0.21875
- dense_content_transform: bfloat16 [2688, 768], replicated, may hold values from -0.125 to 0.125
- dense_respond_transform: bfloat16 [768, 768], replicated, may hold values from -0.21875 to 0.21875
- objective_adjoint: bfloat16 [2, 16384, 768], P(None, 'seq'), may hold values from -6 to 6
Outputs:
- block_out: bfloat16 [2, 16384, 768], P(None, 'seq')
- grad_tokens: float32 [2, 16384, 768], P(None, 'seq')
- grad_first_gain: float32 [768], replicated
- grad_first_bias: float32 [768], replicated
- grad_mix_recept: float32 [768], replicated
- grad_mix_keys: float32 [768], replicated
- grad_mix_values: float32 [768], replicated
- grad_mix_gate: float32 [768], replicated
- grad_recept_weight: float32 [768, 768], replicated
- grad_keys_weight: float32 [768, 768], replicated
- grad_values_weight: float32 [768, 768], replicated
- grad_gate_weight: float32 [768, 768], replicated
- grad_time_decay: float32 [768], replicated
- grad_time_bonus: float32 [768], replicated
- grad_group_gain: float32 [768], replicated
- grad_group_bias: float32 [768], replicated
- grad_output_weight: float32 [768, 768], replicated
- grad_second_gain: float32 [768], replicated
- grad_second_bias: float32 [768], replicated
- grad_mix_expand: float32 [768], replicated
- grad_mix_filter: float32 [768], replicated
- grad_expand_weight: float32 [768, 2688], replicated
- grad_shrink_weight: float32 [2688, 768], replicated
- grad_filter_weight: float32 [768, 768], replicated
Inputs may be any that keep to these rules, and one draw needn't show every extreme that they name: `packed_run_lengths`: each row holds 8 lengths that sum to 16384; the largest of each row is exactly 8192.
All inputs are finite; a program needn't handle non-finite values.
Results may differ from a plain program's by a relative error of at most 0.001.
Values sent between devices are 32-bit elements; how exact they have to be, the bound alone decides.
A program may use at most 512 MiB of HBM per device.

v0:
```python
import functools

import jax
import jax.numpy as jnp
from jax import lax
from jax.experimental import pallas as pl
from jax.experimental.pallas import tpu as pltpu
from jax.sharding import PartitionSpec as P

LANE_FEATURES = 64
PAIR = 2 * LANE_FEATURES
BLOCK = 256
f32 = jnp.float32
bf16 = jnp.bfloat16
VMEM_LIMIT = 60 * 1024 * 1024
MESH = pl.DeviceIdType.MESH


def nothing():
    pass


def split(x):
    high = x.astype(bf16)
    return high, (x - high.astype(f32)).astype(bf16)


def dot(a, b):
    return lax.dot_general(a, b, (((1,), (0,)), ((), ())), preferred_element_type=f32)


def dot_nt(a, b):
    return lax.dot_general(a, b, (((1,), (1,)), ((), ())), preferred_element_type=f32)


def dot_tn(a, b):
    return lax.dot_general(a, b, (((0,), (0,)), ((), ())), preferred_element_type=f32)


def times_weight(x, w):
    high, low = split(x)
    return dot(high, w) + dot(low, w)


def times_weight_t(x, w):
    high, low = split(x)
    return dot_nt(high, w) + dot_nt(low, w)


def outer_sum(a, b):
    ah, al = split(a)
    bh, bl = split(b)
    return dot_tn(ah, bh) + dot_tn(al, bh) + dot_tn(ah, bl)


def standard(x, epsilon=1e-05):
    centred = x - jnp.mean(x, axis=-1, keepdims=True)
    scale = lax.rsqrt(jnp.mean(centred * centred, axis=-1, keepdims=True) + epsilon)
    return centred * scale, scale


def standard_back(grad, normal, scale):
    return scale * (
        grad
        - jnp.mean(grad, axis=-1, keepdims=True)
        - normal * jnp.mean(grad * normal, axis=-1, keepdims=True)
    )


def first_lanes(rows):
    return lax.broadcasted_iota(jnp.int32, (rows, PAIR), 1) < LANE_FEATURES


def head_ones(scale):
    row = lax.broadcasted_iota(jnp.int32, (2 * PAIR, PAIR), 0) // LANE_FEATURES % 2
    col = lax.broadcasted_iota(jnp.int32, (2 * PAIR, PAIR), 1) // LANE_FEATURES
    return jnp.where(row == col, scale, 0.0).astype(bf16)


def head_sum(x, ones):
    return dot(jnp.concatenate(split(x), axis=1), ones)


def widen(state):
    first = first_lanes(LANE_FEATURES)
    return jnp.concatenate([jnp.where(first, state, 0.0), jnp.where(first, 0.0, state)], axis=0)


def compact(square):
    first = first_lanes(LANE_FEATURES)
    return jnp.where(first, square[:LANE_FEATURES], square[LANE_FEATURES:])


def times_state(x, square):
    xh, xl = split(x)
    sh, sl = split(square)
    return dot(jnp.concatenate([xh, xl], axis=1), jnp.concatenate([sh, sh], axis=0)) + dot(xh, sl)


def times_state_t(x, square):
    xh, xl = split(x)
    sh, sl = split(square)
    return dot_nt(jnp.concatenate([xh, xl], axis=1), jnp.concatenate([sh, sh], axis=1)) + dot_nt(xh, sl)


def cut(x):
    high = x.astype(bf16).astype(f32)
    low = x - high
    return high, low, pltpu.roll(high, LANE_FEATURES, 1), pltpu.roll(low, LANE_FEATURES, 1)


def high_low(pieces, first, head):
    high, low, high_r, low_r = pieces
    return (jnp.where(first, high, low_r) if head == 0 else jnp.where(first, high_r, low)).astype(bf16)


def doubled(pieces, first, head):
    high, low, high_r, low_r = pieces
    if head == 0:
        both = (jnp.where(first, high, high_r), jnp.where(first, low, low_r))
    else:
        both = (jnp.where(first, high_r, high), jnp.where(first, low_r, low))
    return jnp.concatenate([part.astype(bf16) for part in both], axis=1)


def twice(x):
    return jnp.concatenate([x, x], axis=1)


def folded(parts, first):
    sums = [part + pltpu.roll(part, LANE_FEATURES, 1) for part in parts]
    return jnp.where(first, sums[0], sums[1])


def decays(log_decay):
    step = lax.broadcasted_iota(jnp.int32, (BLOCK, PAIR), 0).astype(f32)
    return step, jnp.exp(log_decay * step), jnp.exp(-log_decay * (step + 1.0)), jnp.exp(log_decay * BLOCK)


def shifted(normal, row_before, keep):
    rows = lax.broadcasted_iota(jnp.int32, normal.shape, 0)
    return jnp.where(rows == 0, row_before, pltpu.roll(normal, 1, 0)) * keep


GAIN, BIAS, MIX_R, MIX_K, MIX_V, MIX_G, DECAY, BOOST, GROUP_GAIN, GROUP_SHIFT, GAIN2, BIAS2, MIX_E, MIX_F = range(14)


def vec(ref, which, lanes=slice(None)):
    return ref[which : which + 1, lanes]


def bounds_of(lengths_ref, batch):
    at, bounds = jnp.int32(0), []
    for j in range(lengths_ref.shape[1]):
        bounds.append(at)
        at = at + lengths_ref[batch, j]
    return bounds


def segment_of(bounds, position):
    return sum([(position >= bound).astype(jnp.int32) for bound in bounds])


def tokens_kernel(lengths_ref, *refs):
    *vector_refs, cols_ref, row_ref, packed_ref = refs
    for i, ref in enumerate(vector_refs):
        value = ref[...].reshape(1, ref.shape[0])
        packed_ref[i : i + 1] = -jnp.exp(value) if i == DECAY else value
    packed_ref[len(vector_refs) :] = jnp.zeros((2, packed_ref.shape[1]), f32)
    batches, length, columns = cols_ref.shape
    offset = lax.axis_index("seq") * length
    for batch in range(batches):
        bounds = bounds_of(lengths_ref, batch)
        place = offset + lax.broadcasted_iota(jnp.int32, (length, columns), 0)
        segment = segment_of(bounds, place)
        starts = functools.reduce(jnp.logical_or, [place == bound for bound in bounds])
        column = lax.broadcasted_iota(jnp.int32, (length, columns), 1)
        fresh = segment == segment_of(bounds, offset - 1)
        last = segment == segment_of(bounds, offset + length - 1)
        flag = jnp.where(column == 1, jnp.where(starts, 0, 1), jnp.where(column == 2, jnp.where(fresh, 1, 0), jnp.where(last, 1, 0)))
        cols_ref[batch] = jnp.where(column == 0, segment, flag).astype(f32)
        row_ref[batch] = segment_of(bounds, offset + lax.broadcasted_iota(jnp.int32, (1, length), 1)).astype(f32)


def project_kernel(mixes, states, x_ref, before_ref, cols_ref, vec_ref, *refs):
    count = len(mixes)
    weights, outs = refs[:count], refs[count : 2 * count]
    gain, bias = vec(vec_ref, GAIN), vec(vec_ref, BIAS)
    normal = standard(x_ref[0].astype(f32))[0] * gain + bias
    before = standard(before_ref[0])[0] * gain + bias
    earlier = shifted(normal, before, cols_ref[0, :, 1:2])
    difference = normal - earlier
    for mix, weight, out in zip(mixes, weights, outs):
        out[0] = times_weight(earlier + vec(vec_ref, mix) * difference, weight[...])
    if states:
        length, width = normal.shape
        keys, values, end_ref = outs[0], outs[1], refs[2 * count]
        rows = lax.broadcasted_iota(jnp.int32, (length, PAIR), 0).astype(f32)
        for pair in range(width // PAIR):
            lanes = slice(pair * PAIR, (pair + 1) * PAIR)
            tail = jnp.exp(vec(vec_ref, DECAY, lanes) * (length - 1.0 - rows)) * cols_ref[0, :, 3:4]
            end_ref[0, pair] = compact(outer_sum(keys[0, :, lanes] * tail, values[0, :, lanes]))


def allowed_here(cols_ref, row_ref, at, of, across):
    t_col = cols_ref[0, pl.ds(at * BLOCK, BLOCK), 0:1]
    s_row = row_ref[0, :, pl.ds(of * BLOCK, BLOCK)]
    mask = t_col == s_row
    if at == of:
        shape = (BLOCK, BLOCK)
        low, high = (1, 0) if not across else (0, 1)
        mask = jnp.logical_and(
            mask,
            lax.broadcasted_iota(jnp.int32, shape, low) < lax.broadcasted_iota(jnp.int32, shape, high),
        )
    return mask


def mix_kernel(recept_ref, keys_ref, values_ref, cols_ref, row_ref, vec_ref, out_ref):
    length = recept_ref.shape[1]
    log_decay, boost = vec(vec_ref, DECAY), vec(vec_ref, BOOST)
    first = first_lanes(BLOCK)
    step, fall, rise, whole = decays(log_decay)
    ones = head_ones(1.0)
    queries, near, far, values = [], [], [], []
    for at in range(length // BLOCK):
        here = pl.ds(at * BLOCK, BLOCK)
        queries.append(cut(recept_ref[0, here] * fall))
        raised = keys_ref[0, here] * rise
        near.append(cut(raised))
        far.append(raised * whole)
        values.append(cut(values_ref[0, here]))
    for at in range(length // BLOCK):
        here = pl.ds(at * BLOCK, BLOCK)
        totals = [jnp.zeros((BLOCK, PAIR), f32)] * 2
        for of in range(at + 1):
            mask = allowed_here(cols_ref, row_ref, at, of, False)
            gap = jnp.exp(log_decay * (BLOCK * (at - of - 1))) if at > of + 1 else None
            keys = near[of] if of == at else cut(far[of] if gap is None else far[of] * gap)
            for head in range(2):
                scores = dot_nt(twice(high_low(queries[at], first, head)), doubled(keys, first, head))
                sh, sl = split(jnp.where(mask, scores, 0.0))
                held = high_low(values[of], first, head)
                totals[head] = totals[head] + dot(sh, held) + dot(sl, held)
        present = head_sum(recept_ref[0, here] * boost * keys_ref[0, here], ones)
        out_ref[0, here] = folded(totals, first) + present * values_ref[0, here]


def readout_kernel(
    mixed_ref, recept_ref, state_ref, valve_ref, cols_ref, vec_ref, x_ref, weight_ref,
    wkv_ref, attended_ref, second_ref, last_ref,
):
    length, width = mixed_ref.shape[1:]
    rows = lax.broadcasted_iota(jnp.int32, (length, PAIR), 0).astype(f32)
    ones = head_ones(1.0 / LANE_FEATURES)
    fresh = cols_ref[0, :, 2:3]
    gated = []
    for pair in range(width // PAIR):
        lanes = slice(pair * PAIR, (pair + 1) * PAIR)
        query = recept_ref[0, :, lanes] * jnp.exp(vec(vec_ref, DECAY, lanes) * rows) * fresh
        wkv = mixed_ref[0, :, lanes] + times_state(query, widen(state_ref[0, pair]))
        wkv_ref[0, :, lanes] = wkv
        centred = wkv - head_sum(wkv, ones)
        normal = centred * lax.rsqrt(head_sum(centred * centred, ones) + 0.00064)
        grouped = normal * vec(vec_ref, GROUP_GAIN, lanes) + vec(vec_ref, GROUP_SHIFT, lanes)
        gated.append(grouped * jax.nn.silu(valve_ref[0, :, lanes]))
    attended = x_ref[0].astype(f32) + times_weight(jnp.concatenate(gated, axis=1), weight_ref[...])
    attended_ref[0] = attended
    second = standard(attended)[0] * vec(vec_ref, GAIN2) + vec(vec_ref, BIAS2)
    second_ref[0] = second
    last_ref[0] = second[length - 1 :]


def pieces_of(total):
    cuts, at = [], 0
    while at < total:
        size = min(512, total - at)
        cuts.append((at, size))
        at += size
    return cuts


def channel_kernel(low, size, first, last, *refs, tick=nothing):
    refs = list(refs)
    take = lambda count: [refs.pop(0) for _ in range(count)]
    second_ref, ahead_ref, received_ref, grad_ref, cols_ref, vec_ref, expand_any, shrink_any = take(8)
    filter_ref = take(1)[0] if first or last else None
    gate_ref = None if first else take(1)[0]
    total_in, inner_in = (None, None) if first else take(2)
    attended_ref = take(1)[0] if last else None
    gate_out = take(1)[0] if first else None
    if last:
        block_ref, d_second_ref, d_row_ref, d_filter_ref, d_vec_ref = take(5)
    else:
        total_out, inner_out = take(2)
    d_expand_ref, d_shrink_ref, hidden_ref, expand_ref, shrink_ref, sems, carry_ref = refs
    tiles = pl.num_programs(1)
    batch, turn = pl.program_id(0), pl.program_id(1)
    tile = tiles - 1 - turn
    start = jnp.logical_and(batch == 0, turn == 0)

    @pl.when(start)
    def _():
        loads = [
            pltpu.make_async_copy(expand_any.at[:, pl.ds(low, size)], expand_ref, sems.at[0]),
            pltpu.make_async_copy(shrink_any.at[pl.ds(low, size)], shrink_ref, sems.at[1]),
        ]
        for load in loads:
            load.start()
        for ref in [d_expand_ref, d_shrink_ref] + ([d_filter_ref, d_vec_ref] if last else []):
            ref[...] = jnp.zeros_like(ref)
        for load in loads:
            load.wait()

    keep = cols_ref[0, :, 1:2]
    second = second_ref[0]
    before = jnp.where(tile == 0, received_ref[0], ahead_ref[0, 7:8])
    earlier = shifted(second, before, keep)
    difference = second - earlier
    mix_e, mix_f = vec(vec_ref, MIX_E), vec(vec_ref, MIX_F)
    inner_h, inner_l = split(earlier + mix_e * difference)
    if first or last:
        side_h, side_l = split(earlier + mix_f * difference)
    if first:
        gate = jax.nn.sigmoid(dot(side_h, filter_ref[...]) + dot(side_l, filter_ref[...]))
        gate_out[0] = gate
    else:
        gate = gate_ref[0]
    grad = grad_ref[0].astype(f32)
    dt_h, dt_l = split(grad * gate)
    total = jnp.zeros(second.shape, f32) if first else total_in[0]
    d_inner = jnp.zeros(second.shape, f32) if first else inner_in[0]
    for at, wide in pieces_of(size):
        if at:
            tick()
        lanes = slice(at, at + wide)
        raw = jnp.maximum(dot(inner_h, expand_ref[:, lanes]) + dot(inner_l, expand_ref[:, lanes]), 0.0)
        hid_h, hid_l = split(raw * raw)
        total = total + dot(hid_h, shrink_ref[lanes, :]) + dot(hid_l, shrink_ref[lanes, :])
        d_hidden = dot_nt(dt_h, shrink_ref[lanes, :]) + dot_nt(dt_l, shrink_ref[lanes, :])
        dr_h, dr_l = split(d_hidden * (2.0 * raw))
        d_shrink_ref[lanes, :] += dot_tn(hid_h, dt_h) + dot_tn(hid_l, dt_h) + dot_tn(hid_h, dt_l)
        d_expand_ref[:, lanes] += dot_tn(inner_h, dr_h) + dot_tn(inner_l, dr_h) + dot_tn(inner_h, dr_l)
        d_inner = d_inner + dot_nt(dr_h, expand_ref[:, lanes]) + dot_nt(dr_l, expand_ref[:, lanes])
    if not last:
        total_out[0] = total
        inner_out[0] = d_inner
        return
    block_ref[0] = (attended_ref[0] + gate * total).astype(bf16)
    ds_h, ds_l = split(grad * total * (gate * (1.0 - gate)))
    d_filter_ref[...] += dot_tn(side_h, ds_h) + dot_tn(side_l, ds_h) + dot_tn(side_h, ds_l)
    d_side = dot_nt(ds_h, filter_ref[...]) + dot_nt(ds_l, filter_ref[...])
    d_vec_ref[0:1] += jnp.sum(d_inner * difference, axis=0, keepdims=True)
    d_vec_ref[1:2] += jnp.sum(d_side * difference, axis=0, keepdims=True)
    direct = mix_e * d_inner + mix_f * d_side
    passed = (d_inner + d_side - direct) * keep
    rows = lax.broadcasted_iota(jnp.int32, second.shape, 0)
    above = pltpu.roll(passed, second.shape[0] - 1, 0)
    outside = jnp.where(turn == 0, 0.0, carry_ref[...])
    d_second_ref[0] = direct + jnp.where(rows == second.shape[0] - 1, outside, above)
    carry_ref[...] = passed[0:1]
    d_row_ref[0] = passed[0:1]


def attention_back_kernel(
    d_second_ref, back_ref, attended_ref, grad_ref, wkv_ref, valve_ref, recept_ref, cols_ref, vec_ref, weight_ref,
    x_ref, before_ref, d_attended_ref, d_wkv_ref, d_valve_ref, carry_ref, d_weight_ref, d_gate_ref, d_vec_ref,
    tick=nothing,
):
    length, width = attended_ref.shape[1:]

    @pl.when(pl.program_id(0) == 0)
    def _():
        for ref in (d_weight_ref, d_gate_ref, d_vec_ref):
            ref[...] = jnp.zeros_like(ref)

    rows = lax.broadcasted_iota(jnp.int32, (length, width), 0)
    d_second = d_second_ref[0] + jnp.where(rows == length - 1, back_ref[0], 0.0)
    normal2, scale2 = standard(attended_ref[0])
    d_vec_ref[2:3] += jnp.sum(d_second * normal2, axis=0, keepdims=True)
    d_vec_ref[3:4] += jnp.sum(d_second, axis=0, keepdims=True)
    d_attended = grad_ref[0].astype(f32) + standard_back(d_second * vec(vec_ref, GAIN2), normal2, scale2)
    d_attended_ref[0] = d_attended
    d_gated = times_weight_t(d_attended, weight_ref[...])
    steps = lax.broadcasted_iota(jnp.int32, (length, PAIR), 0).astype(f32)
    ones = head_ones(1.0 / LANE_FEATURES)
    fresh = cols_ref[0, :, 2:3]
    gated = []
    for pair in range(width // PAIR):
        lanes = slice(pair * PAIR, (pair + 1) * PAIR)
        wkv = wkv_ref[0, :, lanes]
        centred = wkv - head_sum(wkv, ones)
        scale = lax.rsqrt(head_sum(centred * centred, ones) + 0.00064)
        normal = centred * scale
        grouped = normal * vec(vec_ref, GROUP_GAIN, lanes) + vec(vec_ref, GROUP_SHIFT, lanes)
        valve = valve_ref[0, :, lanes]
        sigmoid = jax.nn.sigmoid(valve)
        gate = valve * sigmoid
        gated.append(grouped * gate)
        d_here = d_gated[:, lanes]
        d_valve_ref[0, :, lanes] = d_here * grouped * (sigmoid * (1.0 + valve * (1.0 - sigmoid)))
        d_grouped = d_here * gate
        d_vec_ref[0:1, lanes] += jnp.sum(d_grouped * normal, axis=0, keepdims=True)
        d_vec_ref[1:2, lanes] += jnp.sum(d_grouped, axis=0, keepdims=True)
        d_normal = d_grouped * vec(vec_ref, GROUP_GAIN, lanes)
        d_wkv = scale * (d_normal - head_sum(d_normal, ones) - normal * head_sum(d_normal * normal, ones))
        d_wkv_ref[0, :, lanes] = d_wkv
        query = recept_ref[0, :, lanes] * jnp.exp(vec(vec_ref, DECAY, lanes) * steps) * fresh
        carry_ref[0, pair] = compact(outer_sum(query, d_wkv))
        if pair == width // PAIR // 2 - 1:
            tick()
    tick()
    d_weight_ref[...] += outer_sum(jnp.concatenate(gated, axis=1), d_attended)
    tick()
    gain, bias = vec(vec_ref, GAIN), vec(vec_ref, BIAS)
    normal = standard(x_ref[0].astype(f32))[0] * gain + bias
    earlier = shifted(normal, standard(before_ref[0])[0] * gain + bias, cols_ref[0, :, 1:2])
    d_gate_ref[...] += outer_sum(earlier + vec(vec_ref, MIX_G) * (normal - earlier), d_valve_ref[0])


def mix_back_kernel(
    recept_ref, keys_ref, values_ref, grad_ref, state_ref, cols_ref, row_ref, vec_ref,
    d_recept_ref, d_keys_ref, d_values_ref, d_vec_ref,
):
    length = recept_ref.shape[1]
    blocks = length // BLOCK
    first = first_lanes(BLOCK)
    log_decay, boost = vec(vec_ref, DECAY), vec(vec_ref, BOOST)
    step, fall, rise, whole = decays(log_decay)
    ones = head_ones(1.0)
    square = widen(state_ref[0, 0])
    queries, near, far, values, grads = [], [], [], [], []
    for at in range(blocks):
        here = pl.ds(at * BLOCK, BLOCK)
        queries.append(cut(recept_ref[0, here] * fall))
        raised = keys_ref[0, here] * rise
        near.append(cut(raised))
        far.append(raised * whole)
        values.append(cut(values_ref[0, here]))
        grads.append(cut(grad_ref[0, here]))
    zero = jnp.zeros((BLOCK, PAIR), f32)
    d_query = [[zero, zero] for _ in range(blocks)]
    d_value = [[zero, zero] for _ in range(blocks)]
    d_near = [[zero, zero] for _ in range(blocks)]
    d_far = [[zero, zero] for _ in range(blocks)]
    for at in range(blocks):
        for of in range(at + 1):
            mask = allowed_here(cols_ref, row_ref, at, of, False)
            t_row = row_ref[0, :, pl.ds(at * BLOCK, BLOCK)]
            s_col = cols_ref[0, pl.ds(of * BLOCK, BLOCK), 0:1]
            mask_t = s_col == t_row
            if at == of:
                shape = (BLOCK, BLOCK)
                mask_t = jnp.logical_and(
                    mask_t, lax.broadcasted_iota(jnp.int32, shape, 0) < lax.broadcasted_iota(jnp.int32, shape, 1)
                )
            gap = jnp.exp(log_decay * (BLOCK * (at - of - 1))) if at > of + 1 else None
            keys = near[of] if of == at else cut(far[of] if gap is None else far[of] * gap)
            for head in range(2):
                q_hl = high_low(queries[at], first, head)
                g_hl = high_low(grads[at], first, head)
                k_hl = high_low(keys, first, head)
                v_hl = high_low(values[of], first, head)
                scores_t = dot_nt(twice(k_hl), doubled(queries[at], first, head))
                s_h, s_l = split(jnp.where(mask_t, scores_t, 0.0))
                d_value[of][head] = d_value[of][head] + dot(s_h, g_hl) + dot(s_l, g_hl)
                d_scores = dot_nt(twice(g_hl), doubled(values[of], first, head))
                s_h, s_l = split(jnp.where(mask, d_scores, 0.0))
                d_query[at][head] = d_query[at][head] + dot(s_h, k_hl) + dot(s_l, k_hl)
                d_scores_t = dot_nt(twice(v_hl), doubled(grads[at], first, head))
                s_h, s_l = split(jnp.where(mask_t, d_scores_t, 0.0))
                d_key = dot(s_h, q_hl) + dot(s_l, q_hl)
                if of == at:
                    d_near[of][head] = d_key
                else:
                    if gap is not None:
                        d_key = d_key * gap
                    d_far[of][head] = d_far[of][head] + d_key
    d_decay = jnp.zeros((1, PAIR), f32)
    d_boost = jnp.zeros((1, PAIR), f32)
    for at in range(blocks):
        here = pl.ds(at * BLOCK, BLOCK)
        recept, keys, value, grad = recept_ref[0, here], keys_ref[0, here], values_ref[0, here], grad_ref[0, here]
        fresh = cols_ref[0, here, 2:3]
        d_in = folded(d_query[at], first) * fall
        d_state = times_state_t(grad, square) * (fall * jnp.exp(log_decay * (BLOCK * at)) * fresh)
        d_here = folded(d_near[at], first) * rise
        d_later = folded(d_far[at], first) * (rise * whole)
        present = head_sum(recept * boost * keys, ones)
        d_present = head_sum(grad * value, ones)
        d_recept_ref[0, here] = d_in + d_state + boost * keys * d_present
        d_keys_ref[0, here] = d_here + d_later + boost * recept * d_present
        d_values_ref[0, here] = folded(d_value[at], first) + present * grad
        d_boost = d_boost + jnp.sum(recept * keys * d_present, axis=0, keepdims=True)
        d_decay = d_decay + jnp.sum(
            recept * (step * d_in + (step + float(BLOCK * at)) * d_state)
            + keys * ((BLOCK - 1.0 - step) * d_later - (step + 1.0) * d_here),
            axis=0,
            keepdims=True,
        )
    d_vec_ref[0, 0:1] = d_decay
    d_vec_ref[0, 1:2] = d_boost


def project_back_kernel(
    x_ref, before_ref, cols_ref, vec_ref, d_attended_ref,
    d_recept_ref, d_keys_ref, d_values_ref, d_valve_ref, keys_ref, values_ref, state_ref, out_state_ref,
    mix_vec_ref, attention_vec_ref, channel_vec_ref, w_r, w_k, w_v, w_g,
    d_x_ref, d_row_ref, packed_ref, dw_r, dw_k, dw_v,
    earlier_ref, difference_ref, direct_ref, passed_ref,
):
    length, width = x_ref.shape[1:]
    turn = pl.program_id(1)
    gain, bias = vec(vec_ref, GAIN), vec(vec_ref, BIAS)
    steps = lax.broadcasted_iota(jnp.int32, (length, PAIR), 0).astype(f32)
    pairs = [(pair, slice(pair * PAIR, (pair + 1) * PAIR)) for pair in range(width // PAIR)]

    @pl.when(jnp.logical_and(pl.program_id(0) == 0, turn == 0))
    def _():
        for ref in (packed_ref, dw_r, dw_k, dw_v):
            ref[...] = jnp.zeros_like(ref)
        packed_ref[GROUP_GAIN : BIAS2 + 1] = attention_vec_ref[...]
        packed_ref[MIX_E : MIX_F + 1] = channel_vec_ref[...]

    def tail_of(lanes):
        return jnp.exp(vec(vec_ref, DECAY, lanes) * (length - 1.0 - steps)) * cols_ref[0, :, 3:4]

    def through(grad, which, weight, d_weight, first=False):
        mix, difference = vec(vec_ref, which), difference_ref[...]
        gh, gl = split(grad)
        if d_weight is not None:
            mh, ml = split(earlier_ref[...] + mix * difference)
            d_weight[...] += dot_tn(mh, gh) + dot_tn(ml, gh) + dot_tn(mh, gl)
        d_mixed = dot_nt(gh, weight[...]) + dot_nt(gl, weight[...])
        packed_ref[which : which + 1] += jnp.sum(d_mixed * difference, axis=0, keepdims=True)
        direct, passed = mix * d_mixed, d_mixed - mix * d_mixed
        direct_ref[...] = direct if first else direct_ref[...] + direct
        passed_ref[...] = passed if first else passed_ref[...] + passed

    @pl.when(turn == 0)
    def _():
        normal = standard(x_ref[0].astype(f32))[0] * gain + bias
        before = standard(before_ref[0])[0] * gain + bias
        earlier = shifted(normal, before, cols_ref[0, :, 1:2])
        earlier_ref[...] = earlier
        difference_ref[...] = normal - earlier
        through(d_recept_ref[0], MIX_R, w_r, dw_r, True)
        packed_ref[DECAY : BOOST + 1] += mix_vec_ref[0]

    @pl.when(turn == 1)
    def _():
        through(d_valve_ref[0], MIX_G, w_g, None)

    @pl.when(turn == 2)
    def _():
        parts = []
        for pair, lanes in pairs:
            d_keys = times_state_t(values_ref[0, :, lanes], widen(out_state_ref[0, pair])) * tail_of(lanes)
            later = (length - 1.0 - steps) * keys_ref[0, :, lanes] * d_keys
            both = widen(state_ref[0, pair]) * widen(out_state_ref[0, pair])
            ones = jnp.ones((8, PAIR), bf16)
            kept = sum([dot_nt(ones, part)[0:1] for part in split(both)])
            kept = kept * jnp.exp(vec(vec_ref, DECAY, lanes) * length) * (float(length) * cols_ref[0, length - 1 :, 2:3])
            packed_ref[DECAY : DECAY + 1, lanes] += jnp.sum(later, axis=0, keepdims=True) + kept
            parts.append(d_keys_ref[0, :, lanes] + d_keys)
        through(jnp.concatenate(parts, axis=1), MIX_K, w_k, dw_k)

    @pl.when(turn == 3)
    def _():
        parts = []
        for pair, lanes in pairs:
            ended = times_state(keys_ref[0, :, lanes] * tail_of(lanes), widen(out_state_ref[0, pair]))
            parts.append(d_values_ref[0, :, lanes] + ended)
        through(jnp.concatenate(parts, axis=1), MIX_V, w_v, dw_v)
        passed = passed_ref[...] * cols_ref[0, :, 1:2]
        rows = lax.broadcasted_iota(jnp.int32, (length, width), 0)
        d_normal = direct_ref[...] + jnp.where(rows == length - 1, 0.0, pltpu.roll(passed, length - 1, 0))
        hat, scale = standard(x_ref[0].astype(f32))
        hat_before, scale_before = standard(before_ref[0])
        out = passed[0:1]
        packed_ref[GAIN : GAIN + 1] += jnp.sum(d_normal * hat, axis=0, keepdims=True) + out * hat_before
        packed_ref[BIAS : BIAS + 1] += jnp.sum(d_normal, axis=0, keepdims=True) + out
        d_x_ref[0] = d_attended_ref[0] + standard_back(d_normal * gain, hat, scale)
        d_row_ref[0] = standard_back(out * gain, hat_before, scale_before)

        @pl.when(pl.program_id(0) == pl.num_programs(0) - 1)
        def _():
            packed_ref[DECAY : DECAY + 1] = packed_ref[DECAY : DECAY + 1] * vec(vec_ref, DECAY)


def call(kernel, grid, ins, outs, name, scratch=(), flops=0, hosts=(), collective_id=None, ticks=1):
    bytes_accessed = sum(a.size * a.dtype.itemsize for a, _, _ in ins)
    for shape, dtype, _, _ in outs:
        size = jnp.dtype(dtype).itemsize
        for extent in shape:
            size *= extent
        bytes_accessed += size

    def spec(block, index):
        if block == "smem":
            return pl.BlockSpec(memory_space=pltpu.SMEM)
        if block == "any":
            return pl.BlockSpec(memory_space=pl.ANY)
        if index is None:
            return pl.BlockSpec(block, lambda *_: (0,) * len(block), pipeline_mode=pl.Buffered(1))
        return pl.BlockSpec(block, index)

    ins, outs, scratch = list(ins), list(outs), list(scratch)
    own, places, aliases = (len(ins), len(outs), len(scratch)), [], {}
    for exchange, _ in hosts:
        more_in, more_out, alias = exchange.operands()
        aliases.update({len(ins) + i: len(outs) + j for i, j in alias})
        place = [len(ins), len(outs), len(scratch)]
        ins, outs, scratch = ins + more_in, outs + more_out, scratch + exchange.scratch()
        places.append([slice(a, b) for a, b in zip(place, (len(ins), len(outs), len(scratch)))])
    steps = 1
    for extent in grid:
        steps *= extent

    def body(*refs):
        in_refs, out_refs, scratch_refs = refs[: len(ins)], refs[len(ins) : len(ins) + len(outs)], refs[len(ins) + len(outs) :]
        step = pl.program_id(0)
        for axis in range(1, len(grid)):
            step = step * grid[axis] + pl.program_id(axis)
        for (exchange, _), (i, o, t) in zip(hosts, places):
            exchange.bind(in_refs[i], out_refs[o], scratch_refs[t])

        def enter():
            barrier = pltpu.get_barrier_semaphore()
            partners = [partner for exchange, _ in hosts for partner in exchange.partners()]
            for partner in partners:
                pl.semaphore_signal(barrier, inc=1, device_id=(partner,), device_id_type=MESH)
            pl.semaphore_wait(barrier, len(partners))
            for exchange, _ in hosts:
                exchange.start()

        def advance(turn):
            for exchange, ends in hosts:
                due = [slot for slot in range(exchange.slots) if min(ends[slot], steps * ticks) == turn]
                if due:

                    @pl.when(step == min(turn // ticks, steps - 1))
                    def _():
                        for slot in due:
                            exchange.run(slot)

        if hosts:
            pl.when(step == 0)(enter)
        for turn in range(steps):
            advance(turn * ticks)
        passed = []

        def tick():
            passed.append(0)
            if len(passed) < ticks:
                for turn in range(steps):
                    advance(turn * ticks + len(passed))

        more = {"tick": tick} if ticks > 1 else {}
        kernel(*in_refs[: own[0]], *out_refs[: own[1]], *scratch_refs[: own[2]], **more)
        advance(steps * ticks)
        if hosts:

            @pl.when(step == steps - 1)
            def _():
                for exchange, _ in hosts:
                    exchange.close()

    params = {"collective_id": collective_id, "has_side_effects": True} if hosts else {}
    return pl.pallas_call(
        body,
        grid=grid,
        in_specs=[spec(block, index) for _, block, index in ins],
        out_specs=[spec(block, index) for _, _, block, index in outs],
        out_shape=[jax.ShapeDtypeStruct(shape, dtype) for shape, dtype, _, _ in outs],
        input_output_aliases=aliases,
        scratch_shapes=scratch,
        compiler_params=pltpu.CompilerParams(
            dimension_semantics=("arbitrary",) * len(grid), vmem_limit_bytes=VMEM_LIMIT, **params
        ),
        cost_estimate=pl.CostEstimate(flops=flops, bytes_accessed=bytes_accessed, transcendentals=0),
        name=name,
    )(*[a for a, _, _ in ins])


def moved(value, steps):
    count = lax.axis_size("seq")
    low, high = max(0, -steps), min(count, count - steps)
    return lax.ppermute(value, "seq", [(source, source + steps) for source in range(low, high)])


def reach(count):
    window, needed, hops = 2, {32: 16, 128: 32}.get(count, count) // 2, []
    while window < needed:
        hops.append(window)
        window *= 2
    return hops


class Carrier:
    def __init__(self, parts, lengths, vectors, length, sign, begin=0, end=None):
        self.count = lax.axis_size("seq")
        self.parts, self.lengths, self.vectors, self.length, self.sign = parts, lengths, vectors, length, sign
        self.hops = [[1, 2]] + [[hop] for hop in reach(self.count)]
        self.whole = len(self.hops) + 2
        self.begin, self.end = begin, self.whole if end is None else end
        self.slots = self.end - self.begin
        batches, pairs = parts[0].shape[:2]
        self.half = pairs // 2 if begin == 0 else pairs
        self.shape = (batches, self.half) + parts[0].shape[2:]

    def operands(self):
        shape = self.shape
        full = (shape[0], 2 * self.half) + shape[2:]
        outs = [(full, f32, full, None)] if self.end == self.whole else [(shape, f32, shape, None)] * 2
        ins = [(part, part.shape, None) for part in self.parts]
        return ins + [(self.vectors, self.vectors.shape, None), (self.lengths, "smem", None)], outs, []

    def scratch(self):
        return [
            pltpu.VMEM((self.slots, 2) + self.shape, f32),
            pltpu.VMEM((self.slots + 1,) + self.shape, f32),
            pltpu.VMEM((2,) + self.shape, f32),
            pltpu.SemaphoreType.DMA((self.slots, 2)),
            pltpu.SemaphoreType.DMA((self.slots, 2)),
        ]

    def bind(self, ins, outs, scratch):
        *self.part_refs, self.vec_ref, self.lengths_ref = ins
        self.out_refs = outs
        self.landed, self.totals, self.kept, self.send_sems, self.recv_sems = scratch
        self.mine = lax.axis_index("seq")
        self.core, self.chip = self.mine % 2, self.mine // 2
        self.sibling = self.mine + 1 - 2 * self.core

    def chip_at(self, hop):
        chips = self.count // 2
        return (self.chip + hop + chips) % chips * 2 + self.core

    def partners(self):
        out = []
        for slot in range(self.begin, self.end):
            if slot in (0, self.whole - 1):
                out.append(self.sibling)
            else:
                out += [self.chip_at(sign * hop) for hop in self.hops[slot - 1] for sign in (1, -1)]
        return out

    def first_part(self):
        return self.kept.at[0] if self.begin == 0 else self.part_refs[1]

    def total(self, slot):
        return self.part_refs[0] if slot == self.begin and slot > 0 else self.totals.at[slot - self.begin]

    def copies(self, slot):
        at = slot - self.begin
        if slot == 0:
            away = self.part_refs[0].at[:, pl.ds((1 - self.core) * self.half, self.half)]
            moves = [(away, self.landed.at[at, 0], self.sibling)]
        elif slot == self.whole - 1:
            moves = [(self.kept.at[1], self.landed.at[at, 0], self.sibling)]
        else:
            moves = [
                (self.total(slot), self.landed.at[at, i], self.chip_at(self.sign * hop))
                for i, hop in enumerate(self.hops[slot - 1])
            ]
        return [
            pltpu.make_async_remote_copy(
                src_ref=source, dst_ref=target, send_sem=self.send_sems.at[at, i], recv_sem=self.recv_sems.at[at, i],
                device_id=(device,), device_id_type=MESH,
            )
            for i, (source, target, device) in enumerate(moves)
        ]

    def start(self):
        self.open(self.begin)

    def open(self, slot):
        if slot == self.whole - 1:
            self.finish()
        for copy in self.copies(slot):
            copy.start()

    def fade(self, pair, devices):
        lane = lax.broadcasted_iota(jnp.int32, (LANE_FEATURES, PAIR), 1)
        row = lax.broadcasted_iota(jnp.int32, (LANE_FEATURES, PAIR), 0)
        at = pl.multiple_of((self.core * self.half + pair) * PAIR, PAIR)
        decay = self.vec_ref[DECAY : DECAY + 1, pl.ds(at, PAIR)] * float(self.length * devices)
        heads = [
            jnp.sum(jnp.where(lane == row + head * LANE_FEATURES, decay, 0.0), axis=1, keepdims=True) for head in range(2)
        ]
        return jnp.exp(jnp.where(first_lanes(LANE_FEATURES), heads[0], heads[1]))

    def same(self, batch, bound, other):
        bounds = bounds_of(self.lengths_ref, batch)
        ends = [segment_of(bounds, (device + 1) * self.length - 1) for device in (bound, other)]
        return jnp.where(ends[0] == ends[1], 1.0, 0.0).astype(f32)

    def edges(self):
        middle = 2 * self.chip
        return middle - self.sign, middle, middle + self.sign

    def run(self, slot):
        slot = slot + self.begin
        at = slot - self.begin
        for copy in self.copies(slot):
            copy.wait()
        batches = self.shape[0]
        entry, middle, leaving = self.edges()
        if slot == 0:
            flags = [self.same(batch, middle, leaving) for batch in range(batches)]
            is_first = self.core == (0 if self.sign > 0 else 1)
            for pair in range(self.half):
                fade = self.fade(pair, 1)
                for batch in range(batches):
                    own = self.part_refs[0][batch, self.core * self.half + pair]
                    other = self.landed[at, 0, batch, pair]
                    ahead, behind = jnp.where(is_first, own, other), jnp.where(is_first, other, own)
                    self.kept[0, batch, pair] = ahead
                    self.totals[at + 1, batch, pair] = ahead * fade * flags[batch] + behind
        elif slot < self.whole - 1:
            hops = self.hops[slot - 1]
            chips = self.count // 2
            flags = []
            for hop in hops:
                there = self.chip - self.sign * hop
                exists = jnp.where(jnp.logical_and(there >= 0, there < chips), 1.0, 0.0).astype(f32)
                crossed = hop - 1 if slot == 1 else hop
                flags.append([exists * self.same(batch, entry - 2 * self.sign * crossed, entry) for batch in range(batches)])
            for pair in range(self.half):
                fade = self.fade(pair, 2 if slot == 1 else 2 * hops[0])
                for batch in range(batches):
                    if slot == 1:
                        near, far = self.landed[at, 0, batch, pair], self.landed[at, 1, batch, pair]
                        here = near * flags[0][batch] + far * fade * flags[1][batch]
                    else:
                        here = self.total(slot)[batch, pair] + self.landed[at, 0, batch, pair] * fade * flags[0][batch]
                    self.totals[at + 1, batch, pair] = here
        else:
            for pair in range(self.half):
                for batch in range(batches):
                    self.out_refs[0][batch, (1 - self.core) * self.half + pair] = self.landed[at, 0, batch, pair]
        if slot + 1 < self.end:
            self.open(slot + 1)
        elif self.end < self.whole:
            self.out_refs[0][...] = self.totals[at + 1]
            self.out_refs[1][...] = self.first_part()[...]

    def close(self):
        pass

    def finish(self):
        entry, middle, _ = self.edges()
        total, first_part = self.total(self.whole - 1), self.first_part()
        is_first = self.core == (0 if self.sign > 0 else 1)
        flags = [self.same(batch, entry, middle) for batch in range(self.shape[0])]
        for pair in range(self.half):
            fade = self.fade(pair, 1)
            for batch in range(self.shape[0]):
                first = total[batch, pair]
                second = first * fade * flags[batch] + first_part[batch, pair]
                self.out_refs[0][batch, self.core * self.half + pair] = jnp.where(is_first, first, second)
                self.kept[1, batch, pair] = jnp.where(is_first, second, first)


def bit_orders(count):
    bits = count.bit_length() - 1
    if bits == 5:
        return [(0, 1, 2, 3, 4), (0, 2, 3, 1, 4), (0, 3, 1, 2, 4)]
    chip = list(range(1, bits))
    third = max(1, len(chip) // 3)
    return [tuple([0] + chip[k * third :] + chip[: k * third]) for k in range(3)]


class Unit:
    def __init__(self, array, first, rows, width, order, group, begin, end):
        self.array, self.first, self.rows, self.width, self.group = array, first, rows, width, group
        self.steps, size, landing = [], rows, 0
        bits = self.bits = len(order)
        for k, bit in enumerate(order):
            halved = size % 16 == 0
            sent = size // 2 if halved else size
            self.steps.append((bit, halved, sent, landing))
            if begin <= k < end:
                landing += sent
            size = sent
        phases = [p for p in range(2 * bits) if p < bits or self.steps[2 * bits - 1 - p][1]]
        self.phases = [p for p in phases if begin <= p < end]
        self.sums = [p for p in self.phases if p < bits]
        self.landing = landing
        self.held = self.steps[self.sums[0]][2] if self.sums else 0
        self.stages = len(self.phases)


def add_rows(target, at, source, source_at, rows):
    block = next(b for b in (64, 56, 48, 32, 24, 16, 8) if rows % b == 0)

    def step(i, _):
        here = pl.ds(pl.multiple_of(at + i * block, 8), block)
        target[here] = target[here] + source[pl.ds(pl.multiple_of(source_at + i * block, 8), block)]
        return 0

    lax.fori_loop(0, rows // block, step, 0)


def rows8(at, size):
    return pl.ds(pl.multiple_of(at, 8), size)


class Summer:
    def __init__(self, arrays, layout):
        self.count, self.arrays, self.units = lax.axis_size("seq"), arrays, []
        orders = bit_orders(self.count)
        for array, first, rows, parts, group, turn, begin, end in layout:
            size = rows // parts
            for part in range(parts):
                order, width = orders[(turn + part) % 3], arrays[array].shape[1]
                self.units.append(Unit(array, first + part * size, size, width, order, group, begin, end))
        self.groups = sorted({unit.group for unit in self.units})
        self.stages = max(unit.stages for unit in self.units)
        self.slots = self.stages + len(self.groups) - 1

    def operands(self):
        arrays = self.arrays
        return (
            [(a, "any", None) for a in arrays],
            [(a.shape, a.dtype, "any", None) for a in arrays],
            [(i, i) for i in range(len(arrays))],
        )

    def scratch(self):
        return (
            [pltpu.VMEM((max(8, unit.held), unit.width), f32) for unit in self.units]
            + [pltpu.VMEM((max(8, unit.landing), unit.width), f32) for unit in self.units]
            + [
                pltpu.SemaphoreType.DMA((len(self.units), self.stages)),
                pltpu.SemaphoreType.DMA((len(self.units), self.stages)),
                pltpu.SemaphoreType.DMA((len(self.units), 2)),
                pltpu.SemaphoreType.REGULAR((len(self.units),)),
            ]
        )

    def bind(self, ins, outs, scratch):
        size = len(self.units)
        self.refs, self.held, self.landed = outs, scratch[:size], scratch[size : 2 * size]
        self.send_sems, self.recv_sems, self.local_sems, self.free_sems = scratch[2 * size :]
        mine = lax.axis_index("seq")
        bits = self.count.bit_length() - 1
        self.bit = [mine // (1 << k) % 2 for k in range(bits)]
        self.partner = [mine + (1 - 2 * self.bit[k]) * (1 << k) for k in range(bits)]
        self.offsets = []
        for unit in self.units:
            at, seen = 0, [0]
            for which, halved, sent, _ in unit.steps:
                at = at + self.bit[which] * sent if halved else at
                seen.append(at)
            self.offsets.append(seen)

    def partners(self):
        used = sorted({unit.steps[min(p, 2 * unit.bits - 1 - p)][0] for unit in self.units for p in unit.phases})
        return [self.partner[k] for k in used]

    def start(self):
        for group in self.groups:
            for u, unit in enumerate(self.units):
                if unit.group == group:
                    self.begin(u, 0)

    def own(self, u, step):
        unit = self.units[u]
        return self.refs[unit.array].at[rows8(unit.first + self.offsets[u][step + 1], unit.steps[step][2])]

    def copies(self, u, stage):
        unit, seen, here = self.units[u], self.offsets[u], self.refs[self.units[u].array]
        phase, out = unit.phases[stage], []
        if phase < unit.bits:
            which, halved, sent, landing = unit.steps[phase]
            away = seen[phase] + (1 - self.bit[which]) * sent if halved else seen[phase]
            target = self.landed[u].at[pl.ds(landing, sent)]
            if stage == 0:
                source = here.at[rows8(unit.first + away, sent)]
                out.append(pltpu.make_async_copy(self.own(u, phase), self.held[u], self.local_sems.at[u, 0]))
            else:
                source = self.held[u].at[rows8(away - seen[unit.sums[0] + 1], sent)]
        else:
            step = 2 * unit.bits - 1 - phase
            which, _, sent, _ = unit.steps[step]
            source = target = self.own(u, step)
            if unit.sums and stage == len(unit.sums):
                source = self.held[u].at[rows8(seen[step + 1] - seen[unit.sums[0] + 1], sent)]
        return out + [
            pltpu.make_async_remote_copy(
                src_ref=source, dst_ref=target, send_sem=self.send_sems.at[u, stage],
                recv_sem=self.recv_sems.at[u, stage], device_id=(self.partner[which],), device_id_type=MESH,
            )
        ]

    def store(self, u):
        unit, seen = self.units[u], self.offsets[u]
        step = unit.sums[-1]
        source = self.held[u].at[rows8(seen[step + 1] - seen[unit.sums[0] + 1], unit.steps[step][2])]
        return pltpu.make_async_copy(source, self.own(u, step), self.local_sems.at[u, 1])

    def returns(self, u):
        unit = self.units[u]
        back = 2 * unit.bits - 1 - unit.phases[0]
        return unit.phases.index(back) if unit.sums and back in unit.phases else None

    def begin(self, u, stage):
        if stage == self.returns(u):
            pl.semaphore_wait(self.free_sems.at[u], 1)
        for copy in self.copies(u, stage):
            copy.start()

    def end(self, u, stage):
        unit, seen = self.units[u], self.offsets[u]
        for copy in self.copies(u, stage):
            copy.wait()
        phase, sums = unit.phases[stage], len(unit.sums)
        if stage == 0 and self.returns(u) is not None:
            partner = self.partner[unit.steps[phase][0]]
            pl.semaphore_signal(self.free_sems.at[u], inc=1, device_id=(partner,), device_id_type=MESH)
        if phase < unit.bits:
            _, _, sent, landing = unit.steps[phase]
            add_rows(self.held[u], seen[phase + 1] - seen[unit.sums[0] + 1], self.landed[u], landing, sent)
            if stage == sums - 1:
                self.store(u).start()
        elif sums and stage == sums:
            self.store(u).wait()

    def close(self):
        for u, unit in enumerate(self.units):
            if unit.sums and unit.stages == len(unit.sums):
                self.store(u).wait()

    def run(self, slot):
        for place, group in enumerate(self.groups):
            for u, unit in enumerate(self.units):
                stage = slot - place
                if unit.group != group:
                    continue
                if unit.phases[0] >= unit.bits and unit.phases[-1] == 2 * unit.bits - 1 and stage >= unit.stages - 1:
                    stage = unit.stages - 1 if slot == self.slots - 1 else -1
                if 0 <= stage < unit.stages:
                    self.end(u, stage)
                    if stage + 1 < unit.stages:
                        self.begin(u, stage + 1)


def summed_over_devices(arrays, layout, collective_id):
    summer = Summer(arrays, layout)
    return call(nothing, (1,), [], [], "sum_over_devices", hosts=[(summer, [1] * summer.slots)], collective_id=collective_id)


def gather_kernel(moves, *refs):
    count = len(moves)
    ins, row_ref, (*outs, sems) = refs[:count], refs[count], refs[count + 1 :]
    buffers, outs = outs[-count:], outs[:-count]
    loads = [pltpu.make_async_copy(source, buffer, sems.at[0, i]) for i, (source, buffer) in enumerate(zip(ins, buffers))]
    for load in loads:
        load.start()
    stores = []
    for i, (out, row, column) in enumerate(moves):
        rows, columns = buffers[i].shape[-2:]
        loads[i].wait()
        if i == count - 1:
            for batch in range(row_ref.shape[0]):
                buffers[i][batch, rows - 1 :] += row_ref[batch]
            stores.append(pltpu.make_async_copy(buffers[i], outs[out], sems.at[1, i]))
            stores[-1].start()
            break
        stores.append(pltpu.make_async_copy(buffers[i], outs[out].at[pl.ds(row, rows), pl.ds(column, columns)], sems.at[1, i]))
        stores[-1].start()
    for store in stores:
        store.wait()


def gathered(arrays, spans, hidden_width, tokens, last_row):
    width = arrays[0].shape[0]
    moves, shapes = [], [(width, hidden_width), (hidden_width, width)]
    for low, _ in spans:
        moves += [(0, 0, low), (1, low, 0)]
    arrays = arrays + [tokens]
    for array in arrays[len(moves) :]:
        moves.append((len(shapes), 0, 0))
        shapes.append(array.shape)
    return call(
        functools.partial(gather_kernel, moves),
        (1,),
        [(a, "any", None) for a in arrays] + [(last_row, last_row.shape, None)],
        [(shape, f32, "any", None) for shape in shapes],
        "gather",
        scratch=[pltpu.VMEM(a.shape, f32) for a in arrays] + [pltpu.SemaphoreType.DMA((2, len(moves)))],
    )


def local(
    incoming_hidden,
    packed_run_lengths,
    prior_standardize_factor,
    prior_standardize_addend,
    respond_interpolant,
    address_interpolant,
    content_interpolant,
    valve_interpolant,
    respond_transform,
    address_transform,
    content_transform,
    valve_transform,
    damping_rates,
    immediate_boost,
    cluster_normal_factor,
    cluster_normal_shift_term,
    readout_transform,
    posterior_standardize_factor,
    posterior_standardize_addend,
    dense_address_interpolant,
    dense_respond_interpolant,
    dense_address_transform,
    dense_content_transform,
    dense_respond_transform,
    objective_adjoint,
):
    batches, length, width = incoming_hidden.shape
    hidden_width = dense_address_transform.shape[1]
    pairs = width // PAIR
    depth = lax.axis_size("seq").bit_length() - 1
    lengths = packed_run_lengths
    vectors = [
        prior_standardize_factor, prior_standardize_addend, respond_interpolant, address_interpolant,
        content_interpolant, valve_interpolant, damping_rates, immediate_boost, cluster_normal_factor,
        cluster_normal_shift_term, posterior_standardize_factor, posterior_standardize_addend,
        dense_address_interpolant, dense_respond_interpolant,
    ]

    def table(w):
        return (w, w.shape, None)

    def rows_of(a):
        return (a, (1,) + a.shape[1:], lambda b, *_: (b,) + (0,) * (a.ndim - 1))

    def rows_out(shape, dtype=f32):
        return (shape, dtype, (1,) + tuple(shape[1:]), lambda b, *_: (b,) + (0,) * (len(shape) - 1))

    def sum_out(*shape):
        return (shape, f32, shape, None)

    tokens, states, one_row = (batches, length, width), (batches, pairs, LANE_FEATURES, PAIR), (batches, 1, width)
    square_flops = 2 * batches * length * width * width
    before = moved(incoming_hidden[:, -1, :].astype(f32), 1)[:, None, :]
    cols, row, vectors = call(
        tokens_kernel,
        (1,),
        [(lengths, "smem", None)] + [table(v) for v in vectors],
        [sum_out(batches, length, 8), sum_out(batches, 1, length), sum_out(16, width)],
        "tokens",
    )
    common = [rows_of(incoming_hidden), rows_of(before), rows_of(cols), table(vectors)]
    keys, values, end_state = call(
        functools.partial(project_kernel, (MIX_K, MIX_V), True),
        (batches,),
        common + [table(address_transform), table(content_transform)],
        [rows_out(tokens)] * 2 + [rows_out(states)],
        "project_keys",
        flops=4 * square_flops,
    )
    nearest = Carrier([end_state], lengths, vectors, length, 1, 0, 2)
    recept, valve, *near_state = call(
        functools.partial(project_kernel, (MIX_R, MIX_G), False),
        (batches,),
        common + [table(respond_transform), table(valve_transform)],
        [rows_out(tokens)] * 2,
        "project_recept",
        flops=4 * square_flops,
        hosts=[(nearest, [batches // 2, batches])],
        collective_id=1,
    )
    by_pair = lambda a: (a, (1, length, PAIR), lambda b, p: (b, 0, p))
    pair_vectors = (vectors, (vectors.shape[0], PAIR), lambda b, p: (0, p))
    pair_state = lambda s: (s, (1, 1, LANE_FEATURES, PAIR), lambda b, p: (b, p, 0, 0))
    pair_out = (tokens, f32, (1, length, PAIR), lambda b, p: (b, 0, p))
    further = Carrier(near_state, lengths, vectors, length, 1, 2)
    steps = batches * pairs
    mixed, state = call(
        mix_kernel,
        (batches, pairs),
        [by_pair(recept), by_pair(keys), by_pair(values), rows_of(cols), rows_of(row), pair_vectors],
        [pair_out],
        "mix",
        flops=3 * 2 * batches * length * length * width * 2,
        hosts=[(further, [(i + 1) * steps // further.slots for i in range(further.slots)])],
        collective_id=2,
    )
    wkv, attended, second, second_row = call(
        readout_kernel,
        (batches,),
        [
            rows_of(mixed), rows_of(recept), rows_of(state), rows_of(valve), rows_of(cols), table(vectors),
            rows_of(incoming_hidden), table(readout_transform),
        ],
        [rows_out(tokens)] * 3 + [rows_out(one_row)],
        "readout",
        flops=2 * square_flops,
    )
    second_row = moved(second_row[:, 0, :], 1)[:, None, :]
    tiles = length // BLOCK
    tile_rows = lambda a: (a, (1, BLOCK, a.shape[2]), lambda b, i: (b, tiles - 1 - i, 0))
    ahead = (second, (1, 8, width), lambda b, i: (b, jnp.maximum((tiles - 1 - i) * (BLOCK // 8) - 1, 0), 0))
    tile_out = lambda dtype: (tokens, dtype, (1, BLOCK, width), lambda b, i: (b, tiles - 1 - i, 0))
    spans = [(at, min(1024, hidden_width - at)) for at in range(0, hidden_width, 1024)]
    ends = 2 * depth

    even = [(0, 0, 128, 0), (0, 128, 128, 1), (0, 256, 512, 2), (1, 0, 512, 0), (1, 512, 512, 1)]
    rest_units = [(2, 0, 768, 0), (0, 0, 768, 1), (1, 0, 512, 2), (1, 512, 128, 2)]
    two = [(0, 0, 512, 0), (0, 512, 256, 2), (1, 0, 512, 1), (1, 512, 256, 2)]

    def layout_of(units, group, begin, end, base=0):
        return [(base + i, first, rows, 1, group, order, begin, end) for i, first, rows, order in units]

    def hosted(arrays, units, begin, end, when):
        summer = Summer(arrays, layout_of(units, 0, begin, end))
        return summer, [when[min(i, len(when) - 1)] for i in range(summer.slots)]

    def channel(part, kept, hosts, collective_id):
        low, size = spans[part]
        first, last = part == 0, part == len(spans) - 1
        ins = [
            tile_rows(second), ahead, rows_of(second_row), tile_rows(objective_adjoint), tile_rows(cols), table(vectors),
            (dense_address_transform, "any", None), (dense_content_transform, "any", None),
        ]
        ins += [table(dense_respond_transform)] if first or last else []
        ins += [tile_rows(a) for a in kept]
        ins += [tile_rows(attended)] if last else []
        if last:
            outs = [tile_out(bf16), tile_out(f32), rows_out(one_row), sum_out(width, width), sum_out(2, width)]
        else:
            outs = [tile_out(f32)] * (3 if first else 2)
        return call(
            functools.partial(channel_kernel, low, size, first, last),
            (batches, tiles),
            ins,
            outs + [sum_out(width, size), sum_out(size, width)],
            "channel_%d" % part,
            scratch=[
                pltpu.VMEM((BLOCK, 8), f32), pltpu.VMEM((width, size), bf16), pltpu.VMEM((size, width), bf16),
                pltpu.SemaphoreType.DMA((2,)), pltpu.VMEM((1, width), f32),
            ],
            flops=7 * 2 * batches * length * width * (2 * size + (width if last else 0)),
            hosts=hosts,
            collective_id=collective_id,
            ticks=2,
        )

    steps = batches * tiles
    gate, total, d_inner, *part_a = channel(0, [], [], None)
    total, d_inner, *rest = channel(1, [gate, total, d_inner], [hosted(part_a, even, 0, 3, [3, 6, 8])], 6)
    part_b, part_a = rest[:2], rest[2:]
    block, d_second, d_second_row, grad_filter, channel_vectors, *rest = channel(
        2,
        [gate, total, d_inner],
        [hosted(part_a, even, 3, depth + 1, [2, 5, 8]), hosted(part_b, even, 0, 2, [3, 8])],
        7,
    )
    part_c, part_a, part_b = [rest[0], rest[1], grad_filter], rest[2:4], rest[4:6]
    back_second = moved(d_second_row[:, 0, :], -1)[:, None, :]
    d_attended, d_wkv, d_valve, carry, grad_output, grad_gate_w, attention_vectors, *rest = call(
        attention_back_kernel,
        (batches,),
        [
            rows_of(d_second), rows_of(back_second), rows_of(attended), rows_of(objective_adjoint), rows_of(wkv),
            rows_of(valve), rows_of(recept), rows_of(cols), table(vectors), table(readout_transform),
            rows_of(incoming_hidden), rows_of(before),
        ],
        [rows_out(tokens)] * 3 + [rows_out(states), sum_out(width, width), sum_out(width, width), sum_out(4, width)],
        "attention_back",
        flops=5 * square_flops,
        hosts=[
            hosted(part_a, even, depth + 1, ends - 2, [2, 5]),
            hosted(part_b, even, 2, depth, [2, 4, 8]),
            hosted(part_c, rest_units, 0, 1, [7]),
        ],
        collective_id=3,
        ticks=4,
    )
    part_a, part_b, part_c, pair = rest[:2], rest[2:4], rest[4:7], [grad_output, grad_gate_w]
    steps = batches * pairs
    arriving = Carrier([carry], lengths, vectors, length, -1)
    d_recept, d_keys, d_values, mix_vectors, out_state, *rest = call(
        mix_back_kernel,
        (batches, pairs),
        [
            by_pair(recept), by_pair(keys), by_pair(values), by_pair(d_wkv), pair_state(state), rows_of(cols), rows_of(row),
            pair_vectors,
        ],
        [pair_out] * 3 + [((batches, 2, width), f32, (1, 2, PAIR), lambda b, p: (b, 0, p))],
        "mix_back",
        flops=9 * 2 * batches * length * length * width * 2,
        hosts=[
            (arriving, [(i + 1) * steps // arriving.slots for i in range(arriving.slots)]),
            hosted(part_b, even, depth, ends - 2, [3, 4, 6]),
            hosted(part_c, rest_units, 1, depth - 1, [4, 7, 9]),
            hosted(part_a, even, ends - 2, ends - 1, [9]),
            hosted(pair, two, 0, 1, [6]),
        ],
        collective_id=4,
    )
    part_b, part_c, part_a, pair = rest[:2], rest[2:5], rest[5:7], rest[7:9]
    wide = lambda: pltpu.VMEM((length, width), f32)
    d_x, d_first_row, packed, grad_recept, grad_keys, grad_values, *rest = call(
        project_back_kernel,
        (batches, 4),
        common
        + [
            rows_of(d_attended), rows_of(d_recept), rows_of(d_keys), rows_of(d_values), rows_of(d_valve),
            rows_of(keys), rows_of(values), rows_of(state), rows_of(out_state), rows_of(mix_vectors),
            table(attention_vectors), table(channel_vectors),
        ]
        + [table(w) for w in (respond_transform, address_transform, content_transform, valve_transform)],
        [rows_out(tokens), rows_out(one_row), sum_out(*vectors.shape)] + [sum_out(width, width)] * 3,
        "project_back",
        scratch=[wide(), wide(), wide(), wide()],
        flops=5 * 4 * square_flops,
        hosts=[
            hosted(part_c, rest_units, depth - 1, depth + 1, [3, 6]),
            hosted(pair, two, 1, depth - 1, [3, 5, 7]),
            hosted(part_b, even, ends - 2, ends - 1, [5]),
            hosted(part_a, even, ends - 1, ends, [8]),
        ],
        collective_id=5,
    )
    part_c, pair, part_b, part_a = rest[:3], rest[3:5], rest[5:7], rest[7:9]
    own = [grad_recept, grad_keys, grad_values]
    layout = layout_of(even, 0, ends - 1, ends) + layout_of(rest_units, 0, depth + 1, ends, 2)
    layout += layout_of(two, 0, depth - 1, ends, 5)
    for half in range(2):
        layout += layout_of([(i, half * width // 2, width // 2, i) for i in range(3)], 1 + half, 0, ends, 7)
    layout += [(10, 0, packed.shape[0], 1, 1, 0, 0, ends)]
    last_row = moved(d_first_row[:, 0, :], -1)[:, None, :]
    summed = summed_over_devices(part_b + part_c + pair + own + [packed], layout, 0)
    w_expand, w_shrink, w_filter, w_output, w_gate, w_recept, w_keys, w_values, vectors, grad_tokens = gathered(
        part_a + list(summed), spans, hidden_width, d_x, last_row
    )
    return (
        block, grad_tokens, *[vectors[i] for i in range(6)], w_recept, w_keys, w_values, w_gate,
        vectors[6], vectors[7], vectors[8], vectors[9], w_output, vectors[10], vectors[11], vectors[12], vectors[13],
        w_expand, w_shrink, w_filter,
    )


def solution(mesh):
    rows = P(None, "seq", None)
    return jax.shard_map(
        local,
        mesh=mesh,
        in_specs=(rows,) + (P(),) * 23 + (rows,),
        out_specs=(rows, rows) + (P(),) * 22,
        check_vma=False,
    )
```

profile of v0, /device:TPU:0, one launch (start us, length us, event | category | flops | bytes accessed | tf_op | source)
XLA Modules:
  0.0 563.3 jit_solution(1410626483088249442)
XLA Ops:
  0.7 0.8 slice.45
  1.4 2.4 collective-permute-start
  3.8 2.4 tokens.1
  6.2 0.0 collective-permute-done
  6.2 0.6 broadcast_in_dim.12.refs_1_.refs_11_
  6.8 10.5 %project_keys.1 = (f32[2,512,768]{2,1,0:T(8,128)}, f32[2,512,768]{2,1,0:T(8,128)}, f32[2,6,64,128]{3,2,1,0:T(8,128)}) custom-call(bf16[2,512,768]{2,1,0:T(8,128)(2,1)} %refs_0_.7, f32[2,1,768]{2,1,0:T(1,128)} %broadcast_in_dim.12.refs_1_.refs_11_, f32[2,512,8]{2,1,0:T(8,128)} %get-tuple-element.126.refs_2_.refs_3_.refs_4_.refs_7_.refs_5_, ...), custom_call_target="tpu_custom_call" | custom-call | flops 4831838208 | bytes 10704896 | tf_op jit(solution)/shard_map/project_keys/pallas_call | solution.py:670
  17.4 25.4 %project_recept.1 = (f32[2,512,768]{2,1,0:T(8,128)}, f32[2,512,768]{2,1,0:T(8,128)}, f32[2,3,64,128]{3,2,1,0:T(8,128)}, f32[2,3,64,128]{3,2,1,0:T(8,128)}) custom-call(bf16[2,512,768]{2,1,0:T(8,128)(2,1)} %refs_0_.7, f32[2,1,768]{2,1,0:T(1,128)} %broadcast_in_dim.12.refs_1_.refs_11_, f32[2,512,8]{2,1,0:T(8,128)} %get-tuple-element.126.refs_2_.refs_3_.refs_4_.refs_7_.refs_5_, ...), custom_call_target="tpu_custom_call" | custom-call | flops 4831838208 | bytes 10311680 | tf_op jit(solution)/shard_map/project_recept/pallas_call | solution.py:670
  42.7 26.0 %mix.1 = (f32[2,512,768]{2,1,0:T(8,128)}, f32[2,6,64,128]{3,2,1,0:T(8,128)}) custom-call(f32[2,512,768]{2,1,0:T(8,128)} %get-tuple-element.129.refs_0_.refs_1_.refs_6_, f32[2,512,768]{2,1,0:T(8,128)} %get-tuple-element.130.refs_1_.refs_9_, f32[2,512,768]{2,1,0:T(8,128)} %get-tuple-element.131.refs_2_.refs_10_, ...), custom_call_target="tpu_custom_call" | custom-call | flops 4831838208 | bytes 12668928 | tf_op jit(solution)/shard_map/mix/pallas_call | solution.py:670
  68.7 14.8 %readout.1 = (f32[2,512,768]{2,1,0:T(8,128)}, f32[2,512,768]{2,1,0:T(8,128)}, f32[2,512,768]{2,1,0:T(8,128)}, f32[2,1,768]{2,1,0:T(1,128)}) custom-call(f32[2,512,768]{2,1,0:T(8,128)} %get-tuple-element.135.refs_0_, f32[2,512,768]{2,1,0:T(8,128)} %get-tuple-element.129.refs_0_.refs_1_.refs_6_, f32[2,6,64,128]{3,2,1,0:T(8,128)} %get-tuple-element.136.refs_2_.refs_4_.refs_11_, ...), custom_call_target="tpu_custom_call" | custom-call | flops 2415919104 | bytes 22108160 | tf_op jit(solution)/shard_map/readout/pallas_call | solution.py:670
  83.6 0.7 copy.104
  84.3 1.7 collective-permute-start.1
  85.9 0.8 collective-permute-done.1
  86.8 0.6 broadcast_in_dim.13.refs_2_
  87.4 36.1 %channel_0.1 = (f32[2,512,768]{2,1,0:T(8,128)}, f32[2,512,768]{2,1,0:T(8,128)}, f32[2,512,768]{2,1,0:T(8,128)}, f32[768,1024]{1,0:T(8,128)}, f32[1024,768]{1,0:T(8,128)}) custom-call(f32[2,512,768]{2,1,0:T(8,128)} %get-tuple-element.138.refs_0_.refs_1_, f32[2,512,768]{2,1,0:T(8,128)} %get-tuple-element.138.refs_0_.refs_1_, ...), custom_call_target="tpu_custom_call" | custom-call | flops 22548578304 | bytes 33118208 | tf_op jit(solution)/shard_map/channel_0/pallas_call | solution.py:670
  123.5 56.8 %channel_1.1 = (f32[2,512,768]{2,1,0:T(8,128)}, f32[2,512,768]{2,1,0:T(8,128)}, f32[768,1024]{1,0:T(8,128)}, f32[1024,768]{1,0:T(8,128)}, f32[768,1024]{1,0:T(8,128)}, /*index=5*/f32[1024,768]{1,0:T(8,128)}) custom-call(f32[2,512,768]{2,1,0:T(8,128)} %get-tuple-element.138.refs_0_.refs_1_, ...), custom_call_target="tpu_custom_call", output_to_operand_aliasing={{4}: (11, {}), {5}: (12, {})} | custom-call | flops 22548578304 | bytes 38230016 | tf_op jit(solution)/shard_map/channel_1/pallas_call | solution.py:670
  180.3 44.4 %channel_2.1 = (bf16[2,512,768]{2,1,0:T(8,128)(2,1)}, f32[2,512,768]{2,1,0:T(8,128)}, f32[2,1,768]{2,1,0:T(1,128)}, f32[768,768]{1,0:T(8,128)}, f32[2,768]{1,0:T...) custom-call(f32[2,512,768]{2,1,0:T(8,128)} %get-tuple-element.138.re, ...), custom_call_target="tpu_custom_call", output_to_operand_aliasing={{7}: (13, {}), {8}: (14, {}), {9}: (15, {}), {10}: (16, {})} | custom-call | flops 22548578304 | bytes 40994816 | tf_op jit(solution)/shard_map/channel_2/pallas_call | solution.py:670
  224.7 0.7 copy.103
  225.4 1.3 collective-permute-start.2
  226.6 1.8 collective-permute-done.2
  228.4 0.6 broadcast_in_dim.14.refs_1_
  229.0 48.3 %attention_back.1 = (f32[2,512,768]{2,1,0:T(8,128)}, f32[2,512,768]{2,1,0:T(8,128)}, f32[2,512,768]{2,1,0:T(8,128)}, f32[2,6,64,128]{3,2,1,0:T(8,128)}, f32[768,...) custom-call(f32[2,512,768]{2,1,0:T(8,128)} %get-tuple-element.153.re, ...), custom_call_target="tpu_custom_call", output_to_operand_aliasing={{7}: (12, {}), {8}: (13, {}), {9}: (14, {}), {10}: (15, {})... | custom-call | flops 6039797760 | bytes 34709504 | tf_op jit(solution)/shard_map/attention_back/pallas_call | solution.py:670
  277.3 88.7 %mix_back.1 = (f32[2,512,768]{2,1,0:T(8,128)}, f32[2,512,768]{2,1,0:T(8,128)}, f32[2,512,768]{2,1,0:T(8,128)}, f32[2,2,768]{2,1,0:T(2,128)}, f32[2,6,64,128]{3,2...) custom-call(f32[2,512,768]{2,1,0:T(8,128)} %get-tuple-element.129.re, ...), custom_call_target="tpu_custom_call", output_to_operand_aliasing={{5}: (11, {}), {6}: (12, {}), {7}: (13, {}), {8}: (14, {}),... | custom-call | flops 14495514624 | bytes 22511616 | tf_op jit(solution)/shard_map/mix_back/pallas_call | solution.py:670
  366.0 58.6 %project_back.1 = (f32[2,512,768]{2,1,0:T(8,128)}, f32[2,1,768]{2,1,0:T(1,128)}, f32[16,768]{1,0:T(8,128)}, f32[768,768]{1,0:T(8,128)}, f32[768,768]{1,0:T(8,128...) custom-call(bf16[2,512,768]{2,1,0:T(8,128)(2,1)} %refs_0_.7, ...), custom_call_target="tpu_custom_call", output_to_operand_aliasing={{6}: (20, {}), {7}: (21, {}), {8}: (22, {}), {9}: (23, {}),... | custom-call | flops 24159191040 | bytes 39495680 | tf_op jit(solution)/shard_map/project_back/pallas_call | solution.py:670
  424.7 0.7 copy.102
  425.4 1.3 collective-permute-start.3
  426.7 108.6 %sum_over_devices.1 = (f32[768,1024]{1,0:T(8,128)}, f32[1024,768]{1,0:T(8,128)}, f32[768,640]{1,0:T(8,128)}, f32[640,768]{1,0:T(8,128)}, f32[768,768]{1,0:T(8,12...) custom-call(f32[768,1024]{1,0:T(8,128)} %get-tuple-element.194.refs_, ...), custom_call_target="tpu_custom_call", output_to_operand_aliasing={{0}: (0, {}), {1}: (1, {}), {2}: (2, {}), {3}: (3, {}), {4}... | custom-call | tf_op jit(solution)/shard_map/sum_over_devices/pallas_call | solution.py:670
  535.3 0.0 collective-permute-done.3
  535.3 0.6 broadcast_in_dim.15.refs_14_
  535.9 24.1 %gather.1 = (f32[768,2688]{1,0:T(8,128)}, f32[2688,768]{1,0:T(8,128)}, f32[768,768]{1,0:T(8,128)}, f32[768,768]{1,0:T(8,128)}, f32[768,768]{1,0:T(8,128)}, /*ind...) custom-call(f32[768,1024]{1,0:T(8,128)} %get-tuple-element.192.refs_, ...), custom_call_target="tpu_custom_call" | custom-call | bytes 67737600 | tf_op jit(solution)/shard_map/gather/pallas_call | solution.py:670
  560.0 1.9 slice_reduce_fusion
  562.0 0.0 copy-done
  562.0 1.1 copy.148
  (2 shorter events, 0.0 us)
Async XLA Ops:
  1.4 4.8 collective-permute-start
  84.3 2.5 collective-permute-start.1
  225.4 3.1 collective-permute-start.2
  425.4 109.9 %collective-permute-start.3 = (f32[2,768]{1,0:T(2,128)S(1)}, f32[2,768]{1,0:T(2,128)S(1)}, u32[]{:S(2)}, u32[]{:S(2)}) collective-permute-start(f32[2,768]{1,0:T(2,128)S(1)} %bitcast.14), channel_id=1, source_target_pairs={{1,0},{2,1},{3,2},{4,3},{5,4},{6,5},{7,6},{8,7},{9,8},{10,9},{11,1... | collective-permute-start | bytes 18440 | tf_op jit(solution)/shard_map/ppermute | solution.py:689
  535.9 26.1 %copy-start = (bf16[2,512,768]{2,1,0:T(8,128)(2,1)S(1)}, bf16[2,512,768]{2,1,0:T(8,128)(2,1)}, u32[]{:S(2)}) copy-start(bf16[2,512,768]{2,1,0:T(8,128)(2,1)} %get-tuple-element.266) | copy-start | bytes 4718596
where the time goes:
time: 567 us; the launch traced here: 563 us
  Pallas kernels  545 us (96%)
  local copies, waits for them, and re-layouts  8.3 us (1%)
  starting transfers between devices  6.59 us (1%)
    pallas_call x13, Pallas kernels, call(): pl.pallas_call(body, grid=grid, in_specs=[spec(block, index) for _, block...  545 us
  transfers between devices with their start and end apart: 4, of which 2 were waited for; matrix products, arithmetic and copies ran while one was open for 0% of the time, Pallas kernels for 20%

commit v1 on v0

--- a/solution.py
+++ b/solution.py
@@ -48,9 +48,16 @@
 
 
 def outer_sum(a, b):
-    ah, al = split(a)
-    bh, bl = split(b)
-    return dot_tn(ah, bh) + dot_tn(al, bh) + dot_tn(ah, bl)
+    return thrice(*split(a), *split(b))
+
+
+def thrice(ah, al, bh, bl):
+    return dot_tn(jnp.concatenate([ah, al, ah], axis=0), jnp.concatenate([bh, bh, bl], axis=0))
+
+
+def both(high, low, w):
+    out = dot(jnp.concatenate([high, low], axis=0), w)
+    return out[: high.shape[0]] + out[high.shape[0] :]
 
 
 def standard(x, epsilon=1e-05):
@@ -241,7 +248,7 @@
                 scores = dot_nt(twice(high_low(queries[at], first, head)), doubled(keys, first, head))
                 sh, sl = split(jnp.where(mask, scores, 0.0))
                 held = high_low(values[of], first, head)
-                totals[head] = totals[head] + dot(sh, held) + dot(sl, held)
+                totals[head] = totals[head] + both(sh, sl, held)
         present = head_sum(recept_ref[0, here] * boost * keys_ref[0, here], ones)
         out_ref[0, here] = folded(totals, first) + present * values_ref[0, here]
 
@@ -251,7 +258,7 @@
     wkv_ref, attended_ref, second_ref, last_ref,
 ):
     length, width = mixed_ref.shape[1:]
-    rows = lax.broadcasted_iota(jnp.int32, (length, PAIR), 0).astype(f32)
+    rows = (pl.program_id(1) * length + lax.broadcasted_iota(jnp.int32, (length, PAIR), 0)).astype(f32)
     ones = head_ones(1.0 / LANE_FEATURES)
     fresh = cols_ref[0, :, 2:3]
     gated = []
@@ -280,7 +287,7 @@
     return cuts
 
 
-def channel_kernel(low, size, first, last, *refs, tick=nothing):
+def channel_kernel(low, size, first, last, *refs):
     refs = list(refs)
     take = lambda count: [refs.pop(0) for _ in range(count)]
     second_ref, ahead_ref, received_ref, grad_ref, cols_ref, vec_ref, expand_any, shrink_any = take(8)
@@ -331,16 +338,14 @@
     total = jnp.zeros(second.shape, f32) if first else total_in[0]
     d_inner = jnp.zeros(second.shape, f32) if first else inner_in[0]
     for at, wide in pieces_of(size):
-        if at:
-            tick()
         lanes = slice(at, at + wide)
         raw = jnp.maximum(dot(inner_h, expand_ref[:, lanes]) + dot(inner_l, expand_ref[:, lanes]), 0.0)
         hid_h, hid_l = split(raw * raw)
         total = total + dot(hid_h, shrink_ref[lanes, :]) + dot(hid_l, shrink_ref[lanes, :])
         d_hidden = dot_nt(dt_h, shrink_ref[lanes, :]) + dot_nt(dt_l, shrink_ref[lanes, :])
         dr_h, dr_l = split(d_hidden * (2.0 * raw))
-        d_shrink_ref[lanes, :] += dot_tn(hid_h, dt_h) + dot_tn(hid_l, dt_h) + dot_tn(hid_h, dt_l)
-        d_expand_ref[:, lanes] += dot_tn(inner_h, dr_h) + dot_tn(inner_l, dr_h) + dot_tn(inner_h, dr_l)
+        d_shrink_ref[lanes, :] += thrice(hid_h, hid_l, dt_h, dt_l)
+        d_expand_ref[:, lanes] += thrice(inner_h, inner_l, dr_h, dr_l)
         d_inner = d_inner + dot_nt(dr_h, expand_ref[:, lanes]) + dot_nt(dr_l, expand_ref[:, lanes])
     if not last:
         total_out[0] = total
@@ -348,7 +353,7 @@
         return
     block_ref[0] = (attended_ref[0] + gate * total).astype(bf16)
     ds_h, ds_l = split(grad * total * (gate * (1.0 - gate)))
-    d_filter_ref[...] += dot_tn(side_h, ds_h) + dot_tn(side_l, ds_h) + dot_tn(side_h, ds_l)
+    d_filter_ref[...] += thrice(side_h, side_l, ds_h, ds_l)
     d_side = dot_nt(ds_h, filter_ref[...]) + dot_nt(ds_l, filter_ref[...])
     d_vec_ref[0:1] += jnp.sum(d_inner * difference, axis=0, keepdims=True)
     d_vec_ref[1:2] += jnp.sum(d_side * difference, axis=0, keepdims=True)
@@ -364,28 +369,27 @@
 
 def attention_back_kernel(
     d_second_ref, back_ref, attended_ref, grad_ref, wkv_ref, valve_ref, recept_ref, cols_ref, vec_ref, weight_ref,
-    x_ref, before_ref, d_attended_ref, d_wkv_ref, d_valve_ref, carry_ref, d_weight_ref, d_gate_ref, d_vec_ref,
-    tick=nothing,
+    d_attended_ref, d_wkv_ref, d_valve_ref, gated_ref, carry_ref, d_vec_ref,
 ):
     length, width = attended_ref.shape[1:]
 
-    @pl.when(pl.program_id(0) == 0)
+    tile, is_last = pl.program_id(1), pl.program_id(1) == pl.num_programs(1) - 1
+
+    @pl.when(jnp.logical_and(pl.program_id(0) == 0, tile == 0))
     def _():
-        for ref in (d_weight_ref, d_gate_ref, d_vec_ref):
-            ref[...] = jnp.zeros_like(ref)
+        d_vec_ref[...] = jnp.zeros_like(d_vec_ref)
 
     rows = lax.broadcasted_iota(jnp.int32, (length, width), 0)
-    d_second = d_second_ref[0] + jnp.where(rows == length - 1, back_ref[0], 0.0)
+    d_second = d_second_ref[0] + jnp.where(jnp.logical_and(rows == length - 1, is_last), back_ref[0], 0.0)
     normal2, scale2 = standard(attended_ref[0])
     d_vec_ref[2:3] += jnp.sum(d_second * normal2, axis=0, keepdims=True)
     d_vec_ref[3:4] += jnp.sum(d_second, axis=0, keepdims=True)
     d_attended = grad_ref[0].astype(f32) + standard_back(d_second * vec(vec_ref, GAIN2), normal2, scale2)
     d_attended_ref[0] = d_attended
     d_gated = times_weight_t(d_attended, weight_ref[...])
-    steps = lax.broadcasted_iota(jnp.int32, (length, PAIR), 0).astype(f32)
+    steps = (tile * length + lax.broadcasted_iota(jnp.int32, (length, PAIR), 0)).astype(f32)
     ones = head_ones(1.0 / LANE_FEATURES)
     fresh = cols_ref[0, :, 2:3]
-    gated = []
     for pair in range(width // PAIR):
         lanes = slice(pair * PAIR, (pair + 1) * PAIR)
         wkv = wkv_ref[0, :, lanes]
@@ -396,7 +400,7 @@
         valve = valve_ref[0, :, lanes]
         sigmoid = jax.nn.sigmoid(valve)
         gate = valve * sigmoid
-        gated.append(grouped * gate)
+        gated_ref[0, :, lanes] = grouped * gate
         d_here = d_gated[:, lanes]
         d_valve_ref[0, :, lanes] = d_here * grouped * (sigmoid * (1.0 + valve * (1.0 - sigmoid)))
         d_grouped = d_here * gate
@@ -406,21 +410,13 @@
         d_wkv = scale * (d_normal - head_sum(d_normal, ones) - normal * head_sum(d_normal * normal, ones))
         d_wkv_ref[0, :, lanes] = d_wkv
         query = recept_ref[0, :, lanes] * jnp.exp(vec(vec_ref, DECAY, lanes) * steps) * fresh
-        carry_ref[0, pair] = compact(outer_sum(query, d_wkv))
-        if pair == width // PAIR // 2 - 1:
-            tick()
-    tick()
-    d_weight_ref[...] += outer_sum(jnp.concatenate(gated, axis=1), d_attended)
-    tick()
-    gain, bias = vec(vec_ref, GAIN), vec(vec_ref, BIAS)
-    normal = standard(x_ref[0].astype(f32))[0] * gain + bias
-    earlier = shifted(normal, standard(before_ref[0])[0] * gain + bias, cols_ref[0, :, 1:2])
-    d_gate_ref[...] += outer_sum(earlier + vec(vec_ref, MIX_G) * (normal - earlier), d_valve_ref[0])
+        carried = compact(outer_sum(query, d_wkv))
+        carry_ref[0, pair] = jnp.where(tile == 0, carried, carry_ref[0, pair] + carried)
 
 
 def mix_back_kernel(
     recept_ref, keys_ref, values_ref, grad_ref, state_ref, cols_ref, row_ref, vec_ref,
-    d_recept_ref, d_keys_ref, d_values_ref, d_vec_ref,
+    gated_ref, d_attended_ref, d_recept_ref, d_keys_ref, d_values_ref, d_vec_ref, d_weight_ref,
 ):
     length = recept_ref.shape[1]
     blocks = length // BLOCK
@@ -456,20 +452,21 @@
                 )
             gap = jnp.exp(log_decay * (BLOCK * (at - of - 1))) if at > of + 1 else None
             keys = near[of] if of == at else cut(far[of] if gap is None else far[of] * gap)
+            mask, mask_t = jnp.where(mask, 1.0, 0.0), jnp.where(mask_t, 1.0, 0.0)
             for head in range(2):
                 q_hl = high_low(queries[at], first, head)
                 g_hl = high_low(grads[at], first, head)
                 k_hl = high_low(keys, first, head)
                 v_hl = high_low(values[of], first, head)
                 scores_t = dot_nt(twice(k_hl), doubled(queries[at], first, head))
-                s_h, s_l = split(jnp.where(mask_t, scores_t, 0.0))
-                d_value[of][head] = d_value[of][head] + dot(s_h, g_hl) + dot(s_l, g_hl)
+                s_h, s_l = split(scores_t * mask_t)
+                d_value[of][head] = d_value[of][head] + both(s_h, s_l, g_hl)
                 d_scores = dot_nt(twice(g_hl), doubled(values[of], first, head))
-                s_h, s_l = split(jnp.where(mask, d_scores, 0.0))
-                d_query[at][head] = d_query[at][head] + dot(s_h, k_hl) + dot(s_l, k_hl)
+                s_h, s_l = split(d_scores * mask)
+                d_query[at][head] = d_query[at][head] + both(s_h, s_l, k_hl)
                 d_scores_t = dot_nt(twice(v_hl), doubled(grads[at], first, head))
-                s_h, s_l = split(jnp.where(mask_t, d_scores_t, 0.0))
-                d_key = dot(s_h, q_hl) + dot(s_l, q_hl)
+                s_h, s_l = split(d_scores_t * mask_t)
+                d_key = both(s_h, s_l, q_hl)
                 if of == at:
                     d_near[of][head] = d_key
                 else:
@@ -500,78 +497,118 @@
         )
     d_vec_ref[0, 0:1] = d_decay
     d_vec_ref[0, 1:2] = d_boost
-
-
-def project_back_kernel(
-    x_ref, before_ref, cols_ref, vec_ref, d_attended_ref,
+    here = rows8(pl.program_id(1) * PAIR, PAIR)
+    d_weight = outer_sum(gated_ref[0], d_attended_ref[0])
+    first_batch = pl.program_id(0) == 0
+
+    @pl.when(first_batch)
+    def _():
+        d_weight_ref[here] = d_weight
+
+    @pl.when(jnp.logical_not(first_batch))
+    def _():
+        d_weight_ref[here] += d_weight
+
+
+def weights_back_kernel(
+    x_ref, before_ref, cols_ref, vec_ref,
     d_recept_ref, d_keys_ref, d_values_ref, d_valve_ref, keys_ref, values_ref, state_ref, out_state_ref,
-    mix_vec_ref, attention_vec_ref, channel_vec_ref, w_r, w_k, w_v, w_g,
-    d_x_ref, d_row_ref, packed_ref, dw_r, dw_k, dw_v,
-    earlier_ref, difference_ref, direct_ref, passed_ref,
+    dw_r, dw_k, dw_v, dw_g, d_keys_out, d_values_out, d_decay_ref, earlier_ref, difference_ref,
 ):
     length, width = x_ref.shape[1:]
     turn = pl.program_id(1)
-    gain, bias = vec(vec_ref, GAIN), vec(vec_ref, BIAS)
     steps = lax.broadcasted_iota(jnp.int32, (length, PAIR), 0).astype(f32)
     pairs = [(pair, slice(pair * PAIR, (pair + 1) * PAIR)) for pair in range(width // PAIR)]
 
     @pl.when(jnp.logical_and(pl.program_id(0) == 0, turn == 0))
     def _():
-        for ref in (packed_ref, dw_r, dw_k, dw_v):
+        for ref in (dw_r, dw_k, dw_v, dw_g, d_decay_ref):
             ref[...] = jnp.zeros_like(ref)
-        packed_ref[GROUP_GAIN : BIAS2 + 1] = attention_vec_ref[...]
-        packed_ref[MIX_E : MIX_F + 1] = channel_vec_ref[...]
 
     def tail_of(lanes):
         return jnp.exp(vec(vec_ref, DECAY, lanes) * (length - 1.0 - steps)) * cols_ref[0, :, 3:4]
 
-    def through(grad, which, weight, d_weight, first=False):
-        mix, difference = vec(vec_ref, which), difference_ref[...]
-        gh, gl = split(grad)
-        if d_weight is not None:
-            mh, ml = split(earlier_ref[...] + mix * difference)
-            d_weight[...] += dot_tn(mh, gh) + dot_tn(ml, gh) + dot_tn(mh, gl)
-        d_mixed = dot_nt(gh, weight[...]) + dot_nt(gl, weight[...])
-        packed_ref[which : which + 1] += jnp.sum(d_mixed * difference, axis=0, keepdims=True)
-        direct, passed = mix * d_mixed, d_mixed - mix * d_mixed
-        direct_ref[...] = direct if first else direct_ref[...] + direct
-        passed_ref[...] = passed if first else passed_ref[...] + passed
+    def weigh(which, grad, d_weight):
+        d_weight[...] += outer_sum(earlier_ref[...] + vec(vec_ref, which) * difference_ref[...], grad)
 
     @pl.when(turn == 0)
     def _():
+        gain, bias = vec(vec_ref, GAIN), vec(vec_ref, BIAS)
         normal = standard(x_ref[0].astype(f32))[0] * gain + bias
         before = standard(before_ref[0])[0] * gain + bias
         earlier = shifted(normal, before, cols_ref[0, :, 1:2])
         earlier_ref[...] = earlier
         difference_ref[...] = normal - earlier
-        through(d_recept_ref[0], MIX_R, w_r, dw_r, True)
-        packed_ref[DECAY : BOOST + 1] += mix_vec_ref[0]
+        weigh(MIX_G, d_valve_ref[0], dw_g)
 
     @pl.when(turn == 1)
     def _():
-        through(d_valve_ref[0], MIX_G, w_g, None)
+        weigh(MIX_R, d_recept_ref[0], dw_r)
 
     @pl.when(turn == 2)
     def _():
-        parts = []
         for pair, lanes in pairs:
             d_keys = times_state_t(values_ref[0, :, lanes], widen(out_state_ref[0, pair])) * tail_of(lanes)
             later = (length - 1.0 - steps) * keys_ref[0, :, lanes] * d_keys
-            both = widen(state_ref[0, pair]) * widen(out_state_ref[0, pair])
+            square = widen(state_ref[0, pair]) * widen(out_state_ref[0, pair])
             ones = jnp.ones((8, PAIR), bf16)
-            kept = sum([dot_nt(ones, part)[0:1] for part in split(both)])
+            kept = sum([dot_nt(ones, part)[0:1] for part in split(square)])
             kept = kept * jnp.exp(vec(vec_ref, DECAY, lanes) * length) * (float(length) * cols_ref[0, length - 1 :, 2:3])
-            packed_ref[DECAY : DECAY + 1, lanes] += jnp.sum(later, axis=0, keepdims=True) + kept
-            parts.append(d_keys_ref[0, :, lanes] + d_keys)
-        through(jnp.concatenate(parts, axis=1), MIX_K, w_k, dw_k)
+            d_decay_ref[:, lanes] += jnp.sum(later, axis=0, keepdims=True) + kept
+            d_keys_out[0, :, lanes] = d_keys_ref[0, :, lanes] + d_keys
+        weigh(MIX_K, d_keys_out[0], dw_k)
 
     @pl.when(turn == 3)
     def _():
-        parts = []
         for pair, lanes in pairs:
             ended = times_state(keys_ref[0, :, lanes] * tail_of(lanes), widen(out_state_ref[0, pair]))
-            parts.append(d_values_ref[0, :, lanes] + ended)
-        through(jnp.concatenate(parts, axis=1), MIX_V, w_v, dw_v)
+            d_values_out[0, :, lanes] = d_values_ref[0, :, lanes] + ended
+        weigh(MIX_V, d_values_out[0], dw_v)
+
+
+def inputs_back_kernel(
+    x_ref, before_ref, cols_ref, vec_ref, d_attended_ref, d_recept_ref, d_keys_ref, d_values_ref, d_valve_ref,
+    mix_vec_ref, attention_vec_ref, channel_vec_ref, d_decay_ref, w_r, w_k, w_v, w_g,
+    d_x_ref, d_row_ref, packed_ref, difference_ref, direct_ref, passed_ref,
+):
+    length, width = x_ref.shape[1:]
+    batch, turn = pl.program_id(0), pl.program_id(1)
+    gain, bias = vec(vec_ref, GAIN), vec(vec_ref, BIAS)
+
+    @pl.when(jnp.logical_and(batch == 0, turn == 0))
+    def _():
+        packed_ref[...] = jnp.zeros_like(packed_ref)
+        packed_ref[GROUP_GAIN : BIAS2 + 1] = attention_vec_ref[...]
+        packed_ref[MIX_E : MIX_F + 1] = channel_vec_ref[...]
+        packed_ref[DECAY : DECAY + 1] = d_decay_ref[...]
+
+    def through(grad, which, weight, first=False):
+        mix = vec(vec_ref, which)
+        d_mixed = times_weight_t(grad, weight[...])
+        packed_ref[which : which + 1] += jnp.sum(d_mixed * difference_ref[...], axis=0, keepdims=True)
+        direct, passed = mix * d_mixed, d_mixed - mix * d_mixed
+        direct_ref[...] = direct if first else direct_ref[...] + direct
+        passed_ref[...] = passed if first else passed_ref[...] + passed
+
+    @pl.when(turn == 0)
+    def _():
+        normal = standard(x_ref[0].astype(f32))[0] * gain + bias
+        before = standard(before_ref[0])[0] * gain + bias
+        difference_ref[...] = normal - shifted(normal, before, cols_ref[0, :, 1:2])
+        packed_ref[DECAY : BOOST + 1] += mix_vec_ref[0]
+        through(d_recept_ref[0], MIX_R, w_r, True)
+
+    @pl.when(turn == 1)
+    def _():
+        through(d_valve_ref[0], MIX_G, w_g)
+
+    @pl.when(turn == 2)
+    def _():
+        through(d_keys_ref[0], MIX_K, w_k)
+
+    @pl.when(turn == 3)
+    def _():
+        through(d_values_ref[0], MIX_V, w_v)
         passed = passed_ref[...] * cols_ref[0, :, 1:2]
         rows = lax.broadcasted_iota(jnp.int32, (length, width), 0)
         d_normal = direct_ref[...] + jnp.where(rows == length - 1, 0.0, pltpu.roll(passed, length - 1, 0))
@@ -581,9 +618,9 @@
         packed_ref[GAIN : GAIN + 1] += jnp.sum(d_normal * hat, axis=0, keepdims=True) + out * hat_before
         packed_ref[BIAS : BIAS + 1] += jnp.sum(d_normal, axis=0, keepdims=True) + out
         d_x_ref[0] = d_attended_ref[0] + standard_back(d_normal * gain, hat, scale)
-        d_row_ref[0] = standard_back(out * gain, hat_before, scale_before)
-
-        @pl.when(pl.program_id(0) == pl.num_programs(0) - 1)
+        d_row_ref[pl.ds(batch, 1)] = standard_back(out * gain, hat_before, scale_before)[None]
+
+        @pl.when(batch == pl.num_programs(0) - 1)
         def _():
             packed_ref[DECAY : DECAY + 1] = packed_ref[DECAY : DECAY + 1] * vec(vec_ref, DECAY)
 
@@ -623,6 +660,7 @@
         for axis in range(1, len(grid)):
             step = step * grid[axis] + pl.program_id(axis)
         for (exchange, _), (i, o, t) in zip(hosts, places):
+            exchange.kernel_outs = out_refs[: own[1]]
             exchange.bind(in_refs[i], out_refs[o], scratch_refs[t])
 
         def enter():
@@ -635,14 +673,17 @@
                 exchange.start()
 
         def advance(turn):
+            due = []
             for exchange, ends in hosts:
-                due = [slot for slot in range(exchange.slots) if min(ends[slot], steps * ticks) == turn]
-                if due:
-
-                    @pl.when(step == min(turn // ticks, steps - 1))
-                    def _():
-                        for slot in due:
-                            exchange.run(slot)
+                slots = [slot for slot in range(exchange.slots) if min(ends[slot], steps * ticks) == turn]
+                due += [((slot + 1) / exchange.slots, exchange, slot) for slot in slots]
+            due.sort(key=lambda entry: entry[0])
+            if due:
+
+                @pl.when(step == min(turn // ticks, steps - 1))
+                def _():
+                    for _, exchange, slot in due:
+                        exchange.run(slot)
 
         if hosts:
             pl.when(step == 0)(enter)
@@ -892,6 +933,65 @@
         self.stages = len(self.phases)
 
 
+class VectorSum:
+    def __init__(self, which, row, shape, row_shape):
+        self.count = lax.axis_size("seq")
+        self.which, self.row, self.shape, self.row_shape = which, row, shape, row_shape
+        self.bits = self.count.bit_length() - 1
+        self.slots = self.bits + 1
+
+    def operands(self):
+        return [], [(self.shape, f32, self.shape, None), (self.row_shape, f32, self.row_shape, None)], []
+
+    def scratch(self):
+        return [
+            pltpu.VMEM((self.bits + 1,) + self.shape, f32), pltpu.VMEM((self.bits,) + self.shape, f32),
+            pltpu.VMEM((2,) + self.row_shape, f32),
+            pltpu.SemaphoreType.DMA((self.bits + 1,)), pltpu.SemaphoreType.DMA((self.bits + 1,)),
+        ]
+
+    def bind(self, ins, outs, scratch):
+        self.out_ref, self.row_ref = outs
+        self.sums, self.landed, self.rows, self.send_sems, self.recv_sems = scratch
+        mine = lax.axis_index("seq")
+        self.partner = [mine + (1 - 2 * (mine // (1 << k) % 2)) * (1 << k) for k in range(self.bits)]
+        self.ahead, self.behind = (mine + self.count - 1) % self.count, (mine + 1) % self.count
+
+    def partners(self):
+        return self.partner + [self.ahead, self.behind]
+
+    def start(self):
+        pass
+
+    def close(self):
+        pass
+
+    def copy(self, k):
+        if k == self.bits:
+            source, target, device = self.rows.at[0], self.rows.at[1], self.ahead
+        else:
+            source, target, device = self.sums.at[k], self.landed.at[k], self.partner[k]
+        return pltpu.make_async_remote_copy(
+            src_ref=source, dst_ref=target, send_sem=self.send_sems.at[k], recv_sem=self.recv_sems.at[k],
+            device_id=(device,), device_id_type=MESH,
+        )
+
+    def run(self, slot):
+        if slot == 0:
+            self.sums[0] = self.kernel_outs[self.which][...]
+            self.rows[0] = self.kernel_outs[self.row][...]
+            self.copy(self.bits).start()
+        else:
+            self.copy(slot - 1).wait()
+            self.sums[slot] = self.sums[slot - 1] + self.landed[slot - 1]
+        if slot < self.bits:
+            self.copy(slot).start()
+        else:
+            self.out_ref[...] = self.sums[slot]
+            self.copy(self.bits).wait()
+            self.row_ref[...] = self.rows[1]
+
+
 def add_rows(target, at, source, source_at, rows):
     block = next(b for b in (64, 56, 48, 32, 24, 16, 8) if rows % b == 0)
 
@@ -915,7 +1015,8 @@
             size = rows // parts
             for part in range(parts):
                 order, width = orders[(turn + part) % 3], arrays[array].shape[1]
-                self.units.append(Unit(array, first + part * size, size, width, order, group, begin, end))
+                unit = Unit(array, first + part * size, size, width, order, group, begin, end)
+                self.units += [unit] if unit.phases else []
         self.groups = sorted({unit.group for unit in self.units})
         self.stages = max(unit.stages for unit in self.units)
         self.slots = self.stages + len(self.groups) - 1
@@ -1045,11 +1146,6 @@
                     self.end(u, stage)
                     if stage + 1 < unit.stages:
                         self.begin(u, stage + 1)
-
-
-def summed_over_devices(arrays, layout, collective_id):
-    summer = Summer(arrays, layout)
-    return call(nothing, (1,), [], [], "sum_over_devices", hosts=[(summer, [1] * summer.slots)], collective_id=collective_id)
 
 
 def gather_kernel(moves, *refs):
@@ -1191,19 +1287,21 @@
         hosts=[(further, [(i + 1) * steps // further.slots for i in range(further.slots)])],
         collective_id=2,
     )
+    tiles = length // BLOCK
+    tiled = lambda a: (a, (1, BLOCK, a.shape[2]), lambda b, i: (b, i, 0))
+    tiled_out = (tokens, f32, (1, BLOCK, width), lambda b, i: (b, i, 0))
     wkv, attended, second, second_row = call(
         readout_kernel,
-        (batches,),
+        (batches, tiles),
         [
-            rows_of(mixed), rows_of(recept), rows_of(state), rows_of(valve), rows_of(cols), table(vectors),
-            rows_of(incoming_hidden), table(readout_transform),
+            tiled(mixed), tiled(recept), rows_of(state), tiled(valve), tiled(cols), table(vectors),
+            tiled(incoming_hidden), table(readout_transform),
         ],
-        [rows_out(tokens)] * 3 + [rows_out(one_row)],
+        [tiled_out] * 3 + [rows_out(one_row)],
         "readout",
         flops=2 * square_flops,
     )
     second_row = moved(second_row[:, 0, :], 1)[:, None, :]
-    tiles = length // BLOCK
     tile_rows = lambda a: (a, (1, BLOCK, a.shape[2]), lambda b, i: (b, tiles - 1 - i, 0))
     ahead = (second, (1, 8, width), lambda b, i: (b, jnp.maximum((tiles - 1 - i) * (BLOCK // 8) - 1, 0), 0))
     tile_out = lambda dtype: (tokens, dtype, (1, BLOCK, width), lambda b, i: (b, tiles - 1 - i, 0))
@@ -1212,7 +1310,7 @@
 
     even = [(0, 0, 128, 0), (0, 128, 128, 1), (0, 256, 512, 2), (1, 0, 512, 0), (1, 512, 512, 1)]
     rest_units = [(2, 0, 768, 0), (0, 0, 768, 1), (1, 0, 512, 2), (1, 512, 128, 2)]
-    two = [(0, 0, 512, 0), (0, 512, 256, 2), (1, 0, 512, 1), (1, 512, 256, 2)]
+    one = [(0, 0, 256, 0), (0, 256, 256, 1), (0, 512, 256, 2)]
 
     def layout_of(units, group, begin, end, base=0):
         return [(base + i, first, rows, 1, group, order, begin, end) for i, first, rows, order in units]
@@ -1248,97 +1346,110 @@
             flops=7 * 2 * batches * length * width * (2 * size + (width if last else 0)),
             hosts=hosts,
             collective_id=collective_id,
-            ticks=2,
         )
 
     steps = batches * tiles
     gate, total, d_inner, *part_a = channel(0, [], [], None)
-    total, d_inner, *rest = channel(1, [gate, total, d_inner], [hosted(part_a, even, 0, 3, [3, 6, 8])], 6)
+    total, d_inner, *rest = channel(1, [gate, total, d_inner], [hosted(part_a, even, 0, 4, [1, 3, 4])], 6)
     part_b, part_a = rest[:2], rest[2:]
     block, d_second, d_second_row, grad_filter, channel_vectors, *rest = channel(
         2,
         [gate, total, d_inner],
-        [hosted(part_a, even, 3, depth + 1, [2, 5, 8]), hosted(part_b, even, 0, 2, [3, 8])],
+        [hosted(part_b, even, 0, 3, [1, 3, 4]), hosted(part_a, even, 4, depth + 2, [2, 3, 4])],
         7,
     )
-    part_c, part_a, part_b = [rest[0], rest[1], grad_filter], rest[2:4], rest[4:6]
+    part_c, part_b, part_a = [rest[0], rest[1], grad_filter], rest[2:4], rest[4:6]
     back_second = moved(d_second_row[:, 0, :], -1)[:, None, :]
-    d_attended, d_wkv, d_valve, carry, grad_output, grad_gate_w, attention_vectors, *rest = call(
+    d_attended, d_wkv, d_valve, gated, carry, attention_vectors, *rest = call(
         attention_back_kernel,
-        (batches,),
+        (batches, tiles),
         [
-            rows_of(d_second), rows_of(back_second), rows_of(attended), rows_of(objective_adjoint), rows_of(wkv),
-            rows_of(valve), rows_of(recept), rows_of(cols), table(vectors), table(readout_transform),
-            rows_of(incoming_hidden), rows_of(before),
+            tiled(d_second), rows_of(back_second), tiled(attended), tiled(objective_adjoint), tiled(wkv),
+            tiled(valve), tiled(recept), tiled(cols), table(vectors), table(readout_transform),
         ],
-        [rows_out(tokens)] * 3 + [rows_out(states), sum_out(width, width), sum_out(width, width), sum_out(4, width)],
+        [tiled_out] * 4 + [rows_out(states), sum_out(4, width)],
         "attention_back",
-        flops=5 * square_flops,
+        flops=2 * square_flops,
         hosts=[
-            hosted(part_a, even, depth + 1, ends - 2, [2, 5]),
-            hosted(part_b, even, 2, depth, [2, 4, 8]),
-            hosted(part_c, rest_units, 0, 1, [7]),
+            hosted(part_c, rest_units, 0, 1, [3]),
+            hosted(part_b, even, 3, depth + 1, [1, 4]),
+            hosted(part_a, even, depth + 2, ends - 1, [2, 4]),
         ],
         collective_id=3,
-        ticks=4,
     )
-    part_a, part_b, part_c, pair = rest[:2], rest[2:4], rest[4:7], [grad_output, grad_gate_w]
+    part_c, part_b, part_a = rest[:3], rest[3:5], rest[5:7]
     steps = batches * pairs
     arriving = Carrier([carry], lengths, vectors, length, -1)
-    d_recept, d_keys, d_values, mix_vectors, out_state, *rest = call(
+    d_recept, d_keys, d_values, mix_vectors, grad_output, out_state, *rest = call(
         mix_back_kernel,
         (batches, pairs),
         [
             by_pair(recept), by_pair(keys), by_pair(values), by_pair(d_wkv), pair_state(state), rows_of(cols), rows_of(row),
-            pair_vectors,
+            pair_vectors, by_pair(gated), rows_of(d_attended),
         ],
-        [pair_out] * 3 + [((batches, 2, width), f32, (1, 2, PAIR), lambda b, p: (b, 0, p))],
+        [pair_out] * 3 + [((batches, 2, width), f32, (1, 2, PAIR), lambda b, p: (b, 0, p)), sum_out(width, width)],
         "mix_back",
         flops=9 * 2 * batches * length * length * width * 2,
         hosts=[
             (arriving, [(i + 1) * steps // arriving.slots for i in range(arriving.slots)]),
-            hosted(part_b, even, depth, ends - 2, [3, 4, 6]),
-            hosted(part_c, rest_units, 1, depth - 1, [4, 7, 9]),
-            hosted(part_a, even, ends - 2, ends - 1, [9]),
-            hosted(pair, two, 0, 1, [6]),
+            hosted(part_b, even, depth + 1, ends - 1, [2, 5, 9]),
+            hosted(part_c, rest_units, 1, depth, [5, 8, 10, 12]),
+            hosted(part_a, even, ends - 1, ends, [6]),
         ],
         collective_id=4,
     )
-    part_b, part_c, part_a, pair = rest[:2], rest[2:5], rest[5:7], rest[7:9]
+    part_b, part_c, part_a = rest[:2], rest[2:5], rest[5:7]
+    steps = 4 * batches
     wide = lambda: pltpu.VMEM((length, width), f32)
-    d_x, d_first_row, packed, grad_recept, grad_keys, grad_values, *rest = call(
-        project_back_kernel,
+    grad_recept, grad_keys, grad_values, grad_gate_w, d_keys, d_values, decay_vector, *rest = call(
+        weights_back_kernel,
+        (batches, 4),
+        common
+        + [
+            rows_of(d_recept), rows_of(d_keys), rows_of(d_values), rows_of(d_valve), rows_of(keys), rows_of(values),
+            rows_of(state), rows_of(out_state),
+        ],
+        [sum_out(width, width)] * 4 + [rows_out(tokens)] * 2 + [sum_out(1, width)],
+        "weights_back",
+        scratch=[wide(), wide()],
+        flops=3 * 4 * square_flops,
+        hosts=[
+            hosted(part_c, rest_units, depth, ends - 2, [4, 6, 8]),
+            hosted([grad_output], one, 0, depth - 1, [2, 4, 6, 8]),
+            hosted(part_b, even, ends - 1, ends, [8]),
+        ],
+        collective_id=5,
+    )
+    part_c, grad_output, part_b = rest[:3], rest[3], rest[4:6]
+    layout, part = [], width // 6
+    for half in range(2):
+        low = half * width // 2
+        layout += layout_of([(i, low, width // 2, i) for i in range(3)], half, 0, ends, 4)
+        layout += layout_of([(3, low + i * part, part, i) for i in range(3)], half, 0, ends, 4)
+    layout += layout_of(rest_units, 2, ends - 2, ends) + layout_of(one, 2, depth - 1, ends, 3)
+    summer = Summer(part_c + [grad_output, grad_recept, grad_keys, grad_values, grad_gate_w], layout)
+    d_x, _, _, *rest = call(
+        inputs_back_kernel,
         (batches, 4),
         common
         + [
             rows_of(d_attended), rows_of(d_recept), rows_of(d_keys), rows_of(d_values), rows_of(d_valve),
-            rows_of(keys), rows_of(values), rows_of(state), rows_of(out_state), rows_of(mix_vectors),
-            table(attention_vectors), table(channel_vectors),
+            rows_of(mix_vectors), table(attention_vectors), table(channel_vectors), table(decay_vector),
         ]
         + [table(w) for w in (respond_transform, address_transform, content_transform, valve_transform)],
-        [rows_out(tokens), rows_out(one_row), sum_out(*vectors.shape)] + [sum_out(width, width)] * 3,
-        "project_back",
-        scratch=[wide(), wide(), wide(), wide()],
-        flops=5 * 4 * square_flops,
+        [rows_out(tokens), sum_out(*one_row), sum_out(*vectors.shape)],
+        "inputs_back",
+        scratch=[wide(), wide(), wide()],
+        flops=2 * 4 * square_flops,
         hosts=[
-            hosted(part_c, rest_units, depth - 1, depth + 1, [3, 6]),
-            hosted(pair, two, 1, depth - 1, [3, 5, 7]),
-            hosted(part_b, even, ends - 2, ends - 1, [5]),
-            hosted(part_a, even, ends - 1, ends, [8]),
+            (summer, [3, 6, 8] + [steps] * (summer.slots - 3)),
+            (VectorSum(2, 1, vectors.shape, one_row), [steps] * (depth + 1)),
         ],
-        collective_id=5,
+        collective_id=0,
     )
-    part_c, pair, part_b, part_a = rest[:3], rest[3:5], rest[5:7], rest[7:9]
-    own = [grad_recept, grad_keys, grad_values]
-    layout = layout_of(even, 0, ends - 1, ends) + layout_of(rest_units, 0, depth + 1, ends, 2)
-    layout += layout_of(two, 0, depth - 1, ends, 5)
-    for half in range(2):
-        layout += layout_of([(i, half * width // 2, width // 2, i) for i in range(3)], 1 + half, 0, ends, 7)
-    layout += [(10, 0, packed.shape[0], 1, 1, 0, 0, ends)]
-    last_row = moved(d_first_row[:, 0, :], -1)[:, None, :]
-    summed = summed_over_devices(part_b + part_c + pair + own + [packed], layout, 0)
-    w_expand, w_shrink, w_filter, w_output, w_gate, w_recept, w_keys, w_values, vectors, grad_tokens = gathered(
-        part_a + list(summed), spans, hidden_width, d_x, last_row
+    summed, vectors, last_row = rest[:8], rest[8], rest[9]
+    w_expand, w_shrink, w_filter, w_output, w_recept, w_keys, w_values, w_gate, grad_tokens = gathered(
+        part_a + part_b + list(summed), spans, hidden_width, d_x, last_row
     )
     return (
         block, grad_tokens, *[vectors[i] for i in range(6)], w_recept, w_keys, w_values, w_gate,

time: 567 us -> 530 us (0.935)
  Pallas kernels: 545 us -> 505 us
    pallas_call x13, Pallas kernels: 545 us -> 505 us  [call(): pl.pallas_call(body, grid=grid, in_specs=[spec(block, index) for _, block...]
  transfers between devices with their start and end apart: 4 -> 3, of which waited for: 2 -> 2; matrix products, arithmetic and copies ran while one was open for 0% -> 0% of each run, Pallas kernels for 20% -> 0%
where the time goes in v1:
time: 530 us; the launch traced here: 521 us
  Pallas kernels  505 us (95%)
  local copies, waits for them, and re-layouts  7.01 us (1%)
    pallas_call x13, Pallas kernels, call(): pl.pallas_call(body, grid=grid, in_specs=[spec(block, index) for _, block...  505 us
  transfers between devices with their start and end apart: 3, of which 2 were waited for; matrix products, arithmetic and copies ran while one was open for 0% of the time, Pallas kernels for 0%

profile of v1, /device:TPU:0, one launch (start us, length us, event | category | flops | bytes accessed | tf_op | source)
XLA Modules:
  0.0 520.9 jit_solution(1919791205889905452)
XLA Ops:
  0.7 0.8 slice.45
  1.4 2.4 collective-permute-start
  3.8 2.4 tokens.1
  6.2 0.0 collective-permute-done
  6.2 0.6 broadcast_in_dim.9.refs_1_
  6.8 10.5 %project_keys.1 = (f32[2,512,768]{2,1,0:T(8,128)}, f32[2,512,768]{2,1,0:T(8,128)}, f32[2,6,64,128]{3,2,1,0:T(8,128)}) custom-call(bf16[2,512,768]{2,1,0:T(8,128)(2,1)} %refs_0_.9, f32[2,1,768]{2,1,0:T(1,128)} %broadcast_in_dim.9.refs_1_, f32[2,512,8]{2,1,0:T(8,128)} %get-tuple-element.121.refs_2_.refs_3_.refs_4_.refs_7_.refs_5_, ...), custom_call_target="tpu_custom_call" | custom-call | flops 4831838208 | bytes 10704896 | tf_op jit(solution)/shard_map/project_keys/pallas_call | solution.py:711
  17.4 25.5 %project_recept.1 = (f32[2,512,768]{2,1,0:T(8,128)}, f32[2,512,768]{2,1,0:T(8,128)}, f32[2,3,64,128]{3,2,1,0:T(8,128)}, f32[2,3,64,128]{3,2,1,0:T(8,128)}) custom-call(bf16[2,512,768]{2,1,0:T(8,128)(2,1)} %refs_0_.9, f32[2,1,768]{2,1,0:T(1,128)} %broadcast_in_dim.9.refs_1_, f32[2,512,8]{2,1,0:T(8,128)} %get-tuple-element.121.refs_2_.refs_3_.refs_4_.refs_7_.refs_5_, ...), custom_call_target="tpu_custom_call" | custom-call | flops 4831838208 | bytes 10311680 | tf_op jit(solution)/shard_map/project_recept/pallas_call | solution.py:711
  42.9 24.0 %mix.1 = (f32[2,512,768]{2,1,0:T(8,128)}, f32[2,6,64,128]{3,2,1,0:T(8,128)}) custom-call(f32[2,512,768]{2,1,0:T(8,128)} %get-tuple-element.124.refs_0_.refs_1_.refs_6_, f32[2,512,768]{2,1,0:T(8,128)} %get-tuple-element.125.refs_1_.refs_8_, f32[2,512,768]{2,1,0:T(8,128)} %get-tuple-element.126.refs_2_.refs_9_, ...), custom_call_target="tpu_custom_call" | custom-call | flops 4831838208 | bytes 12668928 | tf_op jit(solution)/shard_map/mix/pallas_call | solution.py:711
  66.9 15.3 %readout.1 = (f32[2,512,768]{2,1,0:T(8,128)}, f32[2,512,768]{2,1,0:T(8,128)}, f32[2,512,768]{2,1,0:T(8,128)}, f32[2,1,768]{2,1,0:T(1,128)}) custom-call(f32[2,512,768]{2,1,0:T(8,128)} %get-tuple-element.130.refs_0_, f32[2,512,768]{2,1,0:T(8,128)} %get-tuple-element.124.refs_0_.refs_1_.refs_6_, f32[2,6,64,128]{3,2,1,0:T(8,128)} %get-tuple-element.131.refs_2_.refs_4_.refs_10_, ...), custom_call_target="tpu_custom_call" | custom-call | flops 2415919104 | bytes 22108160 | tf_op jit(solution)/shard_map/readout/pallas_call | solution.py:711
  82.2 0.7 copy.93
  82.9 1.5 collective-permute-start.1
  84.4 0.6 collective-permute-done.1
  85.0 0.6 broadcast_in_dim.10.refs_2_
  85.6 35.1 %channel_0.1 = (f32[2,512,768]{2,1,0:T(8,128)}, f32[2,512,768]{2,1,0:T(8,128)}, f32[2,512,768]{2,1,0:T(8,128)}, f32[768,1024]{1,0:T(8,128)}, f32[1024,768]{1,0:T(8,128)}) custom-call(f32[2,512,768]{2,1,0:T(8,128)} %get-tuple-element.133.refs_0_.refs_1_, f32[2,512,768]{2,1,0:T(8,128)} %get-tuple-element.133.refs_0_.refs_1_, ...), custom_call_target="tpu_custom_call" | custom-call | flops 22548578304 | bytes 33118208 | tf_op jit(solution)/shard_map/channel_0/pallas_call | solution.py:711
  120.7 46.0 %channel_1.1 = (f32[2,512,768]{2,1,0:T(8,128)}, f32[2,512,768]{2,1,0:T(8,128)}, f32[768,1024]{1,0:T(8,128)}, f32[1024,768]{1,0:T(8,128)}, f32[768,1024]{1,0:T(8,128)}, /*index=5*/f32[1024,768]{1,0:T(8,128)}) custom-call(f32[2,512,768]{2,1,0:T(8,128)} %get-tuple-element.133.refs_0_.refs_1_, ...), custom_call_target="tpu_custom_call", output_to_operand_aliasing={{4}: (11, {}), {5}: (12, {})} | custom-call | flops 22548578304 | bytes 38230016 | tf_op jit(solution)/shard_map/channel_1/pallas_call | solution.py:711
  166.7 48.2 %channel_2.1 = (bf16[2,512,768]{2,1,0:T(8,128)(2,1)}, f32[2,512,768]{2,1,0:T(8,128)}, f32[2,1,768]{2,1,0:T(1,128)}, f32[768,768]{1,0:T(8,128)}, f32[2,768]{1,0:T...) custom-call(f32[2,512,768]{2,1,0:T(8,128)} %get-tuple-element.133.re, ...), custom_call_target="tpu_custom_call", output_to_operand_aliasing={{7}: (13, {}), {8}: (14, {}), {9}: (15, {}), {10}: (16, {})} | custom-call | flops 22548578304 | bytes 40994816 | tf_op jit(solution)/shard_map/channel_2/pallas_call | solution.py:711
  214.9 0.7 copy.92
  215.6 1.3 collective-permute-start.2
  216.9 1.8 collective-permute-done.2
  218.7 0.6 broadcast_in_dim.11.refs_1_
  219.3 40.8 %attention_back.1 = (f32[2,512,768]{2,1,0:T(8,128)}, f32[2,512,768]{2,1,0:T(8,128)}, f32[2,512,768]{2,1,0:T(8,128)}, f32[2,512,768]{2,1,0:T(8,128)}, f32[2,6,64,...) custom-call(f32[2,512,768]{2,1,0:T(8,128)} %get-tuple-element.148.re, ...), custom_call_target="tpu_custom_call", output_to_operand_aliasing={{6}: (10, {}), {7}: (11, {}), {8}: (12, {}), {9}: (13, {}),... | custom-call | flops 2415919104 | bytes 31557632 | tf_op jit(solution)/shard_map/attention_back/pallas_call | solution.py:711
  260.0 78.5 %mix_back.1 = (f32[2,512,768]{2,1,0:T(8,128)}, f32[2,512,768]{2,1,0:T(8,128)}, f32[2,512,768]{2,1,0:T(8,128)}, f32[2,2,768]{2,1,0:T(2,128)}, f32[768,768]{1,0:T(...) custom-call(f32[2,512,768]{2,1,0:T(8,128)} %get-tuple-element.124.re, ...), custom_call_target="tpu_custom_call", output_to_operand_aliasing={{6}: (13, {}), {7}: (14, {}), {8}: (15, {}), {9}: (16, {}),... | custom-call | flops 14495514624 | bytes 31162368 | tf_op jit(solution)/shard_map/mix_back/pallas_call | solution.py:711
  338.5 39.5 %weights_back.1 = (f32[768,768]{1,0:T(8,128)}, f32[768,768]{1,0:T(8,128)}, f32[768,768]{1,0:T(8,128)}, f32[768,768]{1,0:T(8,128)}, f32[2,512,768]{2,1,0:T(8,128)...) custom-call(bf16[2,512,768]{2,1,0:T(8,128)(2,1)} %refs_0_.9, ...), custom_call_target="tpu_custom_call", output_to_operand_aliasing={{7}: (12, {}), {8}: (13, {}), {9}: (14, {}), {10}: (15, {})... | custom-call | flops 14495514624 | bytes 37053440 | tf_op jit(solution)/shard_map/weights_back/pallas_call | solution.py:711
  378.0 115.2 %inputs_back.1 = (f32[2,512,768]{2,1,0:T(8,128)}, f32[2,1,768]{2,1,0:T(1,128)}, f32[16,768]{1,0:T(8,128)}, f32[768,640]{1,0:T(8,128)}, f32[640,768]{1,0:T(8,128)...) custom-call(bf16[2,512,768]{2,1,0:T(8,128)(2,1)} %refs_0_.9, ...), custom_call_target="tpu_custom_call", output_to_operand_aliasing={{3}: (17, {}), {4}: (18, {}), {5}: (19, {}), {6}: (20, {}),... | custom-call | flops 9663676416 | bytes 25342976 | tf_op jit(solution)/shard_map/inputs_back/pallas_call | solution.py:711
  493.3 1.9 slice_reduce_fusion
  495.2 0.0 copy-start
  495.2 24.1 %gather.1 = (f32[768,2688]{1,0:T(8,128)}, f32[2688,768]{1,0:T(8,128)}, f32[768,768]{1,0:T(8,128)}, f32[768,768]{1,0:T(8,128)}, f32[768,768]{1,0:T(8,128)}, /*ind...) custom-call(f32[768,1024]{1,0:T(8,128)} %get-tuple-element.169.refs_0_, ...), custom_call_target="tpu_custom_call" | custom-call | bytes 67639296 | tf_op jit(solution)/shard_map/gather/pallas_call | solution.py:711
  519.3 0.0 copy-done
  519.3 1.1 copy.129
  (1 shorter events, 0.0 us)
Async XLA Ops:
  1.4 4.8 collective-permute-start
  82.9 2.1 collective-permute-start.1
  215.6 3.1 collective-permute-start.2
  495.2 24.1 %copy-start = (bf16[2,512,768]{2,1,0:T(8,128)(2,1)S(1)}, bf16[2,512,768]{2,1,0:T(8,128)(2,1)}, u32[]{:S(2)}) copy-start(bf16[2,512,768]{2,1,0:T(8,128)(2,1)} %get-tuple-element.256) | copy-start | bytes 4718596

commit v2 on v1

--- a/solution.py
+++ b/solution.py
@@ -281,13 +281,13 @@
 def pieces_of(total):
     cuts, at = [], 0
     while at < total:
-        size = min(512, total - at)
+        size = min(1024, total - at)
         cuts.append((at, size))
         at += size
     return cuts
 
 
-def channel_kernel(low, size, first, last, *refs):
+def channel_kernel(low, size, first, last, shift, *refs):
     refs = list(refs)
     take = lambda count: [refs.pop(0) for _ in range(count)]
     second_ref, ahead_ref, received_ref, grad_ref, cols_ref, vec_ref, expand_any, shrink_any = take(8)
@@ -321,7 +321,8 @@
 
     keep = cols_ref[0, :, 1:2]
     second = second_ref[0]
-    before = jnp.where(tile == 0, received_ref[0], ahead_ref[0, 7:8])
+    received = received_ref[0] if shift is None else shift.out_ref[pl.ds(batch, 1)][0]
+    before = jnp.where(tile == 0, received, ahead_ref[0, 7:8])
     earlier = shifted(second, before, keep)
     difference = second - earlier
     mix_e, mix_f = vec(vec_ref, MIX_E), vec(vec_ref, MIX_F)
@@ -364,7 +365,7 @@
     outside = jnp.where(turn == 0, 0.0, carry_ref[...])
     d_second_ref[0] = direct + jnp.where(rows == second.shape[0] - 1, outside, above)
     carry_ref[...] = passed[0:1]
-    d_row_ref[0] = passed[0:1]
+    d_row_ref[pl.ds(batch, 1)] = passed[0:1][None]
 
 
 def attention_back_kernel(
@@ -933,6 +934,53 @@
         self.stages = len(self.phases)
 
 
+class RowShift:
+    def __init__(self, shape, hops, row=None, which=None):
+        self.count, self.shape, self.hops, self.row, self.which = lax.axis_size("seq"), shape, hops, row, which
+        self.slots = 1 if which is None else 2
+
+    def operands(self):
+        ins = [(self.row, self.shape, None)] if self.which is None else []
+        return ins, [(self.shape, f32, self.shape, None)], []
+
+    def scratch(self):
+        return [pltpu.VMEM((2,) + self.shape, f32), pltpu.SemaphoreType.DMA, pltpu.SemaphoreType.DMA]
+
+    def bind(self, ins, outs, scratch):
+        self.in_refs, (self.out_ref,) = ins, outs
+        self.rows, self.send_sem, self.recv_sem = scratch
+        mine = lax.axis_index("seq")
+        self.sent_to, self.got_from = (mine + self.hops + self.count) % self.count, mine - self.hops
+
+    def partners(self):
+        return [self.sent_to, (self.got_from + self.count) % self.count]
+
+    def copy(self):
+        return pltpu.make_async_remote_copy(
+            src_ref=self.rows.at[0], dst_ref=self.rows.at[1], send_sem=self.send_sem, recv_sem=self.recv_sem,
+            device_id=(self.sent_to,), device_id_type=MESH,
+        )
+
+    def send(self, source):
+        self.rows[0] = source[...]
+        self.copy().start()
+
+    def start(self):
+        if self.which is None:
+            self.send(self.in_refs[0])
+
+    def run(self, slot):
+        if slot < self.slots - 1:
+            self.send(self.kernel_outs[self.which])
+        else:
+            self.copy().wait()
+            inside = jnp.logical_and(self.got_from >= 0, self.got_from < self.count)
+            self.out_ref[...] = jnp.where(inside, self.rows[1], 0.0)
+
+    def close(self):
+        pass
+
+
 class VectorSum:
     def __init__(self, which, row, shape, row_shape):
         self.count = lax.axis_size("seq")
@@ -1150,11 +1198,13 @@
 
 def gather_kernel(moves, *refs):
     count = len(moves)
-    ins, row_ref, (*outs, sems) = refs[:count], refs[count], refs[count + 1 :]
+    ins, row_ref, vectors_ref, (*outs, sems) = refs[:count], refs[count], refs[count + 1], refs[count + 2 :]
     buffers, outs = outs[-count:], outs[:-count]
     loads = [pltpu.make_async_copy(source, buffer, sems.at[0, i]) for i, (source, buffer) in enumerate(zip(ins, buffers))]
     for load in loads:
         load.start()
+    for i, ref in enumerate(outs[moves[-1][0] + 1 :]):
+        ref[...] = vectors_ref[i : i + 1].reshape(ref.shape)
     stores = []
     for i, (out, row, column) in enumerate(moves):
         rows, columns = buffers[i].shape[-2:]
@@ -1171,7 +1221,7 @@
         store.wait()
 
 
-def gathered(arrays, spans, hidden_width, tokens, last_row):
+def gathered(arrays, spans, hidden_width, tokens, last_row, vectors, count):
     width = arrays[0].shape[0]
     moves, shapes = [], [(width, hidden_width), (hidden_width, width)]
     for low, _ in spans:
@@ -1183,8 +1233,8 @@
     return call(
         functools.partial(gather_kernel, moves),
         (1,),
-        [(a, "any", None) for a in arrays] + [(last_row, last_row.shape, None)],
-        [(shape, f32, "any", None) for shape in shapes],
+        [(a, "any", None) for a in arrays] + [(last_row, last_row.shape, None), (vectors, vectors.shape, None)],
+        [(shape, f32, "any", None) for shape in shapes] + [((width,), f32, (width,), None)] * count,
         "gather",
         scratch=[pltpu.VMEM(a.shape, f32) for a in arrays] + [pltpu.SemaphoreType.DMA((2, len(moves)))],
     )
@@ -1301,7 +1351,6 @@
         "readout",
         flops=2 * square_flops,
     )
-    second_row = moved(second_row[:, 0, :], 1)[:, None, :]
     tile_rows = lambda a: (a, (1, BLOCK, a.shape[2]), lambda b, i: (b, tiles - 1 - i, 0))
     ahead = (second, (1, 8, width), lambda b, i: (b, jnp.maximum((tiles - 1 - i) * (BLOCK // 8) - 1, 0), 0))
     tile_out = lambda dtype: (tokens, dtype, (1, BLOCK, width), lambda b, i: (b, tiles - 1 - i, 0))
@@ -1319,7 +1368,7 @@
         summer = Summer(arrays, layout_of(units, 0, begin, end))
         return summer, [when[min(i, len(when) - 1)] for i in range(summer.slots)]
 
-    def channel(part, kept, hosts, collective_id):
+    def channel(part, kept, hosts, collective_id, shift=None):
         low, size = spans[part]
         first, last = part == 0, part == len(spans) - 1
         ins = [
@@ -1330,11 +1379,11 @@
         ins += [tile_rows(a) for a in kept]
         ins += [tile_rows(attended)] if last else []
         if last:
-            outs = [tile_out(bf16), tile_out(f32), rows_out(one_row), sum_out(width, width), sum_out(2, width)]
+            outs = [tile_out(bf16), tile_out(f32), sum_out(*one_row), sum_out(width, width), sum_out(2, width)]
         else:
             outs = [tile_out(f32)] * (3 if first else 2)
         return call(
-            functools.partial(channel_kernel, low, size, first, last),
+            functools.partial(channel_kernel, low, size, first, last, shift),
             (batches, tiles),
             ins,
             outs + [sum_out(width, size), sum_out(size, width)],
@@ -1349,17 +1398,17 @@
         )
 
     steps = batches * tiles
-    gate, total, d_inner, *part_a = channel(0, [], [], None)
+    shift = RowShift(one_row, 1, second_row)
+    gate, total, d_inner, *part_a, second_row = channel(0, [], [(shift, [1])], 8, shift)
     total, d_inner, *rest = channel(1, [gate, total, d_inner], [hosted(part_a, even, 0, 4, [1, 3, 4])], 6)
     part_b, part_a = rest[:2], rest[2:]
-    block, d_second, d_second_row, grad_filter, channel_vectors, *rest = channel(
+    block, d_second, _, grad_filter, channel_vectors, *rest = channel(
         2,
         [gate, total, d_inner],
-        [hosted(part_b, even, 0, 3, [1, 3, 4]), hosted(part_a, even, 4, depth + 2, [2, 3, 4])],
+        [hosted(part_b, even, 0, 3, [1, 3, 4]), hosted(part_a, even, 4, depth + 2, [2, 3, 4]), (RowShift(one_row, -1, which=2), [steps] * 2)],
         7,
     )
-    part_c, part_b, part_a = [rest[0], rest[1], grad_filter], rest[2:4], rest[4:6]
-    back_second = moved(d_second_row[:, 0, :], -1)[:, None, :]
+    part_c, part_b, part_a, back_second = [rest[0], rest[1], grad_filter], rest[2:4], rest[4:6], rest[6]
     d_attended, d_wkv, d_valve, gated, carry, attention_vectors, *rest = call(
         attention_back_kernel,
         (batches, tiles),
@@ -1414,19 +1463,19 @@
         scratch=[wide(), wide()],
         flops=3 * 4 * square_flops,
         hosts=[
-            hosted(part_c, rest_units, depth, ends - 2, [4, 6, 8]),
-            hosted([grad_output], one, 0, depth - 1, [2, 4, 6, 8]),
+            hosted([grad_output], one, 0, depth, [1, 3, 4, 6, 8]),
+            hosted(part_c, rest_units, depth, ends - 1, [3, 4, 6, 8]),
             hosted(part_b, even, ends - 1, ends, [8]),
         ],
         collective_id=5,
     )
-    part_c, grad_output, part_b = rest[:3], rest[3], rest[4:6]
+    grad_output, part_c, part_b = rest[0], rest[1:4], rest[4:6]
     layout, part = [], width // 6
     for half in range(2):
         low = half * width // 2
-        layout += layout_of([(i, low, width // 2, i) for i in range(3)], half, 0, ends, 4)
+        layout += layout_of([(i, low, width // 2, (i + half) % 3) for i in range(3)], half, 0, ends, 4)
         layout += layout_of([(3, low + i * part, part, i) for i in range(3)], half, 0, ends, 4)
-    layout += layout_of(rest_units, 2, ends - 2, ends) + layout_of(one, 2, depth - 1, ends, 3)
+    layout += layout_of(rest_units, 2, ends - 1, ends) + layout_of(one, 2, depth, ends, 3)
     summer = Summer(part_c + [grad_output, grad_recept, grad_keys, grad_values, grad_gate_w], layout)
     d_x, _, _, *rest = call(
         inputs_back_kernel,
@@ -1448,8 +1497,8 @@
         collective_id=0,
     )
     summed, vectors, last_row = rest[:8], rest[8], rest[9]
-    w_expand, w_shrink, w_filter, w_output, w_recept, w_keys, w_values, w_gate, grad_tokens = gathered(
-        part_a + part_b + list(summed), spans, hidden_width, d_x, last_row
+    w_expand, w_shrink, w_filter, w_output, w_recept, w_keys, w_values, w_gate, grad_tokens, *vectors = gathered(
+        part_a + part_b + list(summed), spans, hidden_width, d_x, last_row, vectors, MIX_F + 1
     )
     return (
         block, grad_tokens, *[vectors[i] for i in range(6)], w_recept, w_keys, w_values, w_gate,

time: 530 us -> 515 us (0.972)
  transfers between devices with their start and end apart: 3 -> 1, of which waited for: 2 -> 0; matrix products, arithmetic and copies ran while one was open for 0% -> 0% of each run, Pallas kernels for 0% -> 0%
where the time goes in v2:
time: 515 us; the launch traced here: 506 us
  Pallas kernels  500 us (97%)
    pallas_call x13, Pallas kernels, call(): pl.pallas_call(body, grid=grid, in_specs=[spec(block, index) for _, block...  500 us
  transfers between devices with their start and end apart: 1, of which 0 were waited for; matrix products, arithmetic and copies ran while one was open for 0% of the time, Pallas kernels for 0%

profile of v2, /device:TPU:0, one launch (start us, length us, event | category | flops | bytes accessed | tf_op | source)
XLA Modules:
  0.0 506.0 jit_solution(12095637010786190090)
XLA Ops:
  0.7 0.8 slice.3
  1.4 2.4 collective-permute-start
  3.8 2.4 tokens.1
  6.2 0.0 collective-permute-done
  6.2 0.6 broadcast_in_dim.3.refs_1_
  6.8 10.5 %project_keys.1 = (f32[2,512,768]{2,1,0:T(8,128)}, f32[2,512,768]{2,1,0:T(8,128)}, f32[2,6,64,128]{3,2,1,0:T(8,128)}) custom-call(bf16[2,512,768]{2,1,0:T(8,128)(2,1)} %refs_0_.9, f32[2,1,768]{2,1,0:T(1,128)} %broadcast_in_dim.3.refs_1_, f32[2,512,8]{2,1,0:T(8,128)} %get-tuple-element.136.refs_2_.refs_3_.refs_4_.refs_7_.refs_5_, ...), custom_call_target="tpu_custom_call" | custom-call | flops 4831838208 | bytes 10704896 | tf_op jit(solution)/shard_map/project_keys/pallas_call | solution.py:712
  17.4 25.5 %project_recept.1 = (f32[2,512,768]{2,1,0:T(8,128)}, f32[2,512,768]{2,1,0:T(8,128)}, f32[2,3,64,128]{3,2,1,0:T(8,128)}, f32[2,3,64,128]{3,2,1,0:T(8,128)}) custom-call(bf16[2,512,768]{2,1,0:T(8,128)(2,1)} %refs_0_.9, f32[2,1,768]{2,1,0:T(1,128)} %broadcast_in_dim.3.refs_1_, f32[2,512,8]{2,1,0:T(8,128)} %get-tuple-element.136.refs_2_.refs_3_.refs_4_.refs_7_.refs_5_, ...), custom_call_target="tpu_custom_call" | custom-call | flops 4831838208 | bytes 10311680 | tf_op jit(solution)/shard_map/project_recept/pallas_call | solution.py:712
  42.9 24.0 %mix.1 = (f32[2,512,768]{2,1,0:T(8,128)}, f32[2,6,64,128]{3,2,1,0:T(8,128)}) custom-call(f32[2,512,768]{2,1,0:T(8,128)} %get-tuple-element.139.refs_0_.refs_1_.refs_6_, f32[2,512,768]{2,1,0:T(8,128)} %get-tuple-element.140.refs_1_.refs_8_, f32[2,512,768]{2,1,0:T(8,128)} %get-tuple-element.141.refs_2_.refs_9_, ...), custom_call_target="tpu_custom_call" | custom-call | flops 4831838208 | bytes 12668928 | tf_op jit(solution)/shard_map/mix/pallas_call | solution.py:712
  66.9 15.3 %readout.1 = (f32[2,512,768]{2,1,0:T(8,128)}, f32[2,512,768]{2,1,0:T(8,128)}, f32[2,512,768]{2,1,0:T(8,128)}, f32[2,1,768]{2,1,0:T(1,128)}) custom-call(f32[2,512,768]{2,1,0:T(8,128)} %get-tuple-element.145.refs_0_, f32[2,512,768]{2,1,0:T(8,128)} %get-tuple-element.139.refs_0_.refs_1_.refs_6_, f32[2,6,64,128]{3,2,1,0:T(8,128)} %get-tuple-element.146.refs_2_.refs_4_.refs_10_, ...), custom_call_target="tpu_custom_call" | custom-call | flops 2415919104 | bytes 22108160 | tf_op jit(solution)/shard_map/readout/pallas_call | solution.py:712
  82.1 36.3 %channel_0.1 = (f32[2,512,768]{2,1,0:T(8,128)}, f32[2,512,768]{2,1,0:T(8,128)}, f32[2,512,768]{2,1,0:T(8,128)}, f32[768,1024]{1,0:T(8,128)}, f32[1024,768]{1,0:T(8,128)}, /*index=5*/f32[2,1,768]{2,1,0:T(1,128)}) custom-call(f32[2,512,768]{2,1,0:T(8,128)} %get-tuple-element.148.refs_0_.refs_1_, f32[2,512,768]{2,1,0:T(8,128)} %get-tuple-element.148.refs_0_.refs_1_, ...), custom_call_target="tpu_custom_call" | custom-call | flops 22548578304 | bytes 33118208 | tf_op jit(solution)/shard_map/channel_0/pallas_call | solution.py:712
  118.4 41.2 %channel_1.1 = (f32[2,512,768]{2,1,0:T(8,128)}, f32[2,512,768]{2,1,0:T(8,128)}, f32[768,1024]{1,0:T(8,128)}, f32[1024,768]{1,0:T(8,128)}, f32[768,1024]{1,0:T(8,128)}, /*index=5*/f32[1024,768]{1,0:T(8,128)}) custom-call(f32[2,512,768]{2,1,0:T(8,128)} %get-tuple-element.148.refs_0_.refs_1_, ...), custom_call_target="tpu_custom_call", output_to_operand_aliasing={{4}: (11, {}), {5}: (12, {})} | custom-call | flops 22548578304 | bytes 38230016 | tf_op jit(solution)/shard_map/channel_1/pallas_call | solution.py:712
  159.6 46.6 %channel_2.1 = (bf16[2,512,768]{2,1,0:T(8,128)(2,1)}, f32[2,512,768]{2,1,0:T(8,128)}, f32[2,1,768]{2,1,0:T(1,128)}, f32[768,768]{1,0:T(8,128)}, f32[2,768]{1,0:T...) custom-call(f32[2,512,768]{2,1,0:T(8,128)} %get-tuple-element.148.re, ...), custom_call_target="tpu_custom_call", output_to_operand_aliasing={{7}: (13, {}), {8}: (14, {}), {9}: (15, {}), {10}: (16, {})} | custom-call | flops 22548578304 | bytes 40994816 | tf_op jit(solution)/shard_map/channel_2/pallas_call | solution.py:712
  206.2 39.5 %attention_back.1 = (f32[2,512,768]{2,1,0:T(8,128)}, f32[2,512,768]{2,1,0:T(8,128)}, f32[2,512,768]{2,1,0:T(8,128)}, f32[2,512,768]{2,1,0:T(8,128)}, f32[2,6,64,...) custom-call(f32[2,512,768]{2,1,0:T(8,128)} %get-tuple-element.164.re, ...), custom_call_target="tpu_custom_call", output_to_operand_aliasing={{6}: (10, {}), {7}: (11, {}), {8}: (12, {}), {9}: (13, {}),... | custom-call | flops 2415919104 | bytes 31557632 | tf_op jit(solution)/shard_map/attention_back/pallas_call | solution.py:712
  245.8 77.5 %mix_back.1 = (f32[2,512,768]{2,1,0:T(8,128)}, f32[2,512,768]{2,1,0:T(8,128)}, f32[2,512,768]{2,1,0:T(8,128)}, f32[2,2,768]{2,1,0:T(2,128)}, f32[768,768]{1,0:T(...) custom-call(f32[2,512,768]{2,1,0:T(8,128)} %get-tuple-element.139.re, ...), custom_call_target="tpu_custom_call", output_to_operand_aliasing={{6}: (13, {}), {7}: (14, {}), {8}: (15, {}), {9}: (16, {}),... | custom-call | flops 14495514624 | bytes 31162368 | tf_op jit(solution)/shard_map/mix_back/pallas_call | solution.py:712
  323.3 50.3 %weights_back.1 = (f32[768,768]{1,0:T(8,128)}, f32[768,768]{1,0:T(8,128)}, f32[768,768]{1,0:T(8,128)}, f32[768,768]{1,0:T(8,128)}, f32[2,512,768]{2,1,0:T(8,128)...) custom-call(bf16[2,512,768]{2,1,0:T(8,128)(2,1)} %refs_0_.9, ...), custom_call_target="tpu_custom_call", output_to_operand_aliasing={{7}: (12, {}), {8}: (13, {}), {9}: (14, {}), {10}: (15, {})... | custom-call | flops 14495514624 | bytes 37053440 | tf_op jit(solution)/shard_map/weights_back/pallas_call | solution.py:712
  373.6 106.1 %inputs_back.1 = (f32[2,512,768]{2,1,0:T(8,128)}, f32[2,1,768]{2,1,0:T(1,128)}, f32[16,768]{1,0:T(8,128)}, f32[768,640]{1,0:T(8,128)}, f32[640,768]{1,0:T(8,128)...) custom-call(bf16[2,512,768]{2,1,0:T(8,128)(2,1)} %refs_0_.9, ...), custom_call_target="tpu_custom_call", output_to_operand_aliasing={{3}: (17, {}), {4}: (18, {}), {5}: (19, {}), {6}: (20, {}),... | custom-call | flops 9663676416 | bytes 25342976 | tf_op jit(solution)/shard_map/inputs_back/pallas_call | solution.py:712
  479.8 0.0 copy-start
  479.8 24.9 %gather.1 = (f32[768,2688]{1,0:T(8,128)}, f32[2688,768]{1,0:T(8,128)}, f32[768,768]{1,0:T(8,128)}, f32[768,768]{1,0:T(8,128)}, f32[768,768]{1,0:T(8,128)}, /*ind...) custom-call(f32[768,1024]{1,0:T(8,128)} %get-tuple-element.185.refs_, ...), custom_call_target="tpu_custom_call" | custom-call | bytes 67731456 | tf_op jit(solution)/shard_map/gather/pallas_call | solution.py:712
  504.7 0.0 copy-done
  504.7 1.1 copy.123
  (1 shorter events, 0.0 us)
Async XLA Ops:
  1.4 4.8 collective-permute-start
  479.8 24.9 %copy-start = (bf16[2,512,768]{2,1,0:T(8,128)(2,1)S(1)}, bf16[2,512,768]{2,1,0:T(8,128)(2,1)}, u32[]{:S(2)}) copy-start(bf16[2,512,768]{2,1,0:T(8,128)(2,1)} %get-tuple-element.272) | copy-start | bytes 4718596

commit v3 on v2

--- a/solution.py
+++ b/solution.py
@@ -370,7 +370,7 @@
 
 def attention_back_kernel(
     d_second_ref, back_ref, attended_ref, grad_ref, wkv_ref, valve_ref, recept_ref, cols_ref, vec_ref, weight_ref,
-    d_attended_ref, d_wkv_ref, d_valve_ref, gated_ref, carry_ref, d_vec_ref,
+    d_attended_ref, d_wkv_ref, d_valve_ref, carry_ref, d_weight_ref, d_vec_ref,
 ):
     length, width = attended_ref.shape[1:]
 
@@ -379,6 +379,7 @@
     @pl.when(jnp.logical_and(pl.program_id(0) == 0, tile == 0))
     def _():
         d_vec_ref[...] = jnp.zeros_like(d_vec_ref)
+        d_weight_ref[...] = jnp.zeros_like(d_weight_ref)
 
     rows = lax.broadcasted_iota(jnp.int32, (length, width), 0)
     d_second = d_second_ref[0] + jnp.where(jnp.logical_and(rows == length - 1, is_last), back_ref[0], 0.0)
@@ -391,6 +392,7 @@
     steps = (tile * length + lax.broadcasted_iota(jnp.int32, (length, PAIR), 0)).astype(f32)
     ones = head_ones(1.0 / LANE_FEATURES)
     fresh = cols_ref[0, :, 2:3]
+    gated = []
     for pair in range(width // PAIR):
         lanes = slice(pair * PAIR, (pair + 1) * PAIR)
         wkv = wkv_ref[0, :, lanes]
@@ -401,7 +403,7 @@
         valve = valve_ref[0, :, lanes]
         sigmoid = jax.nn.sigmoid(valve)
         gate = valve * sigmoid
-        gated_ref[0, :, lanes] = grouped * gate
+        gated.append(grouped * gate)
         d_here = d_gated[:, lanes]
         d_valve_ref[0, :, lanes] = d_here * grouped * (sigmoid * (1.0 + valve * (1.0 - sigmoid)))
         d_grouped = d_here * gate
@@ -413,11 +415,12 @@
         query = recept_ref[0, :, lanes] * jnp.exp(vec(vec_ref, DECAY, lanes) * steps) * fresh
         carried = compact(outer_sum(query, d_wkv))
         carry_ref[0, pair] = jnp.where(tile == 0, carried, carry_ref[0, pair] + carried)
+    d_weight_ref[...] += outer_sum(jnp.concatenate(gated, axis=1), d_attended)
 
 
 def mix_back_kernel(
     recept_ref, keys_ref, values_ref, grad_ref, state_ref, cols_ref, row_ref, vec_ref,
-    gated_ref, d_attended_ref, d_recept_ref, d_keys_ref, d_values_ref, d_vec_ref, d_weight_ref,
+    d_recept_ref, d_keys_ref, d_values_ref, d_vec_ref,
 ):
     length = recept_ref.shape[1]
     blocks = length // BLOCK
@@ -498,17 +501,6 @@
         )
     d_vec_ref[0, 0:1] = d_decay
     d_vec_ref[0, 1:2] = d_boost
-    here = rows8(pl.program_id(1) * PAIR, PAIR)
-    d_weight = outer_sum(gated_ref[0], d_attended_ref[0])
-    first_batch = pl.program_id(0) == 0
-
-    @pl.when(first_batch)
-    def _():
-        d_weight_ref[here] = d_weight
-
-    @pl.when(jnp.logical_not(first_batch))
-    def _():
-        d_weight_ref[here] += d_weight
 
 
 def weights_back_kernel(
@@ -1409,14 +1401,14 @@
         7,
     )
     part_c, part_b, part_a, back_second = [rest[0], rest[1], grad_filter], rest[2:4], rest[4:6], rest[6]
-    d_attended, d_wkv, d_valve, gated, carry, attention_vectors, *rest = call(
+    d_attended, d_wkv, d_valve, carry, grad_output, attention_vectors, *rest = call(
         attention_back_kernel,
         (batches, tiles),
         [
             tiled(d_second), rows_of(back_second), tiled(attended), tiled(objective_adjoint), tiled(wkv),
             tiled(valve), tiled(recept), tiled(cols), table(vectors), table(readout_transform),
         ],
-        [tiled_out] * 4 + [rows_out(states), sum_out(4, width)],
+        [tiled_out] * 3 + [rows_out(states), sum_out(width, width), sum_out(4, width)],
         "attention_back",
         flops=2 * square_flops,
         hosts=[
@@ -1429,14 +1421,14 @@
     part_c, part_b, part_a = rest[:3], rest[3:5], rest[5:7]
     steps = batches * pairs
     arriving = Carrier([carry], lengths, vectors, length, -1)
-    d_recept, d_keys, d_values, mix_vectors, grad_output, out_state, *rest = call(
+    d_recept, d_keys, d_values, mix_vectors, out_state, *rest = call(
         mix_back_kernel,
         (batches, pairs),
         [
             by_pair(recept), by_pair(keys), by_pair(values), by_pair(d_wkv), pair_state(state), rows_of(cols), rows_of(row),
-            pair_vectors, by_pair(gated), rows_of(d_attended),
+            pair_vectors,
         ],
-        [pair_out] * 3 + [((batches, 2, width), f32, (1, 2, PAIR), lambda b, p: (b, 0, p)), sum_out(width, width)],
+        [pair_out] * 3 + [((batches, 2, width), f32, (1, 2, PAIR), lambda b, p: (b, 0, p))],
         "mix_back",
         flops=9 * 2 * batches * length * length * width * 2,
         hosts=[

time: 515 us -> 513 us (level)
  no operation moved by 1% of the time
where the time goes in v3:
time: 513 us; the launch traced here: 504 us
  Pallas kernels  498 us (97%)
    pallas_call x13, Pallas kernels, call(): pl.pallas_call(body, grid=grid, in_specs=[spec(block, index) for _, block...  498 us
  transfers between devices with their start and end apart: 1, of which 0 were waited for; matrix products, arithmetic and copies ran while one was open for 0% of the time, Pallas kernels for 0%

profile of v3, /device:TPU:0, one launch (start us, length us, event | category | flops | bytes accessed | tf_op | source)
XLA Modules:
  0.0 504.0 jit_solution(4795409511489674965)
XLA Ops:
  0.7 0.8 slice.3
  1.4 2.4 collective-permute-start
  3.8 2.4 tokens.1
  6.2 0.0 collective-permute-done
  6.2 0.6 broadcast_in_dim.3.refs_1_
  6.8 10.5 %project_keys.1 = (f32[2,512,768]{2,1,0:T(8,128)}, f32[2,512,768]{2,1,0:T(8,128)}, f32[2,6,64,128]{3,2,1,0:T(8,128)}) custom-call(bf16[2,512,768]{2,1,0:T(8,128)(2,1)} %refs_0_.9, f32[2,1,768]{2,1,0:T(1,128)} %broadcast_in_dim.3.refs_1_, f32[2,512,8]{2,1,0:T(8,128)} %get-tuple-element.135.refs_2_.refs_3_.refs_4_.refs_7_.refs_5_, ...), custom_call_target="tpu_custom_call" | custom-call | flops 4831838208 | bytes 10704896 | tf_op jit(solution)/shard_map/project_keys/pallas_call | solution.py:704
  17.4 25.5 %project_recept.1 = (f32[2,512,768]{2,1,0:T(8,128)}, f32[2,512,768]{2,1,0:T(8,128)}, f32[2,3,64,128]{3,2,1,0:T(8,128)}, f32[2,3,64,128]{3,2,1,0:T(8,128)}) custom-call(bf16[2,512,768]{2,1,0:T(8,128)(2,1)} %refs_0_.9, f32[2,1,768]{2,1,0:T(1,128)} %broadcast_in_dim.3.refs_1_, f32[2,512,8]{2,1,0:T(8,128)} %get-tuple-element.135.refs_2_.refs_3_.refs_4_.refs_7_.refs_5_, ...), custom_call_target="tpu_custom_call" | custom-call | flops 4831838208 | bytes 10311680 | tf_op jit(solution)/shard_map/project_recept/pallas_call | solution.py:704
  42.9 24.0 %mix.1 = (f32[2,512,768]{2,1,0:T(8,128)}, f32[2,6,64,128]{3,2,1,0:T(8,128)}) custom-call(f32[2,512,768]{2,1,0:T(8,128)} %get-tuple-element.138.refs_0_.refs_1_.refs_6_, f32[2,512,768]{2,1,0:T(8,128)} %get-tuple-element.139.refs_1_.refs_8_, f32[2,512,768]{2,1,0:T(8,128)} %get-tuple-element.140.refs_2_.refs_9_, ...), custom_call_target="tpu_custom_call" | custom-call | flops 4831838208 | bytes 12668928 | tf_op jit(solution)/shard_map/mix/pallas_call | solution.py:704
  66.9 15.3 %readout.1 = (f32[2,512,768]{2,1,0:T(8,128)}, f32[2,512,768]{2,1,0:T(8,128)}, f32[2,512,768]{2,1,0:T(8,128)}, f32[2,1,768]{2,1,0:T(1,128)}) custom-call(f32[2,512,768]{2,1,0:T(8,128)} %get-tuple-element.144.refs_0_, f32[2,512,768]{2,1,0:T(8,128)} %get-tuple-element.138.refs_0_.refs_1_.refs_6_, f32[2,6,64,128]{3,2,1,0:T(8,128)} %get-tuple-element.145.refs_2_.refs_4_.refs_10_, ...), custom_call_target="tpu_custom_call" | custom-call | flops 2415919104 | bytes 22108160 | tf_op jit(solution)/shard_map/readout/pallas_call | solution.py:704
  82.1 36.0 %channel_0.1 = (f32[2,512,768]{2,1,0:T(8,128)}, f32[2,512,768]{2,1,0:T(8,128)}, f32[2,512,768]{2,1,0:T(8,128)}, f32[768,1024]{1,0:T(8,128)}, f32[1024,768]{1,0:T(8,128)}, /*index=5*/f32[2,1,768]{2,1,0:T(1,128)}) custom-call(f32[2,512,768]{2,1,0:T(8,128)} %get-tuple-element.147.refs_0_.refs_1_, f32[2,512,768]{2,1,0:T(8,128)} %get-tuple-element.147.refs_0_.refs_1_, ...), custom_call_target="tpu_custom_call" | custom-call | flops 22548578304 | bytes 33118208 | tf_op jit(solution)/shard_map/channel_0/pallas_call | solution.py:704
  118.2 41.1 %channel_1.1 = (f32[2,512,768]{2,1,0:T(8,128)}, f32[2,512,768]{2,1,0:T(8,128)}, f32[768,1024]{1,0:T(8,128)}, f32[1024,768]{1,0:T(8,128)}, f32[768,1024]{1,0:T(8,128)}, /*index=5*/f32[1024,768]{1,0:T(8,128)}) custom-call(f32[2,512,768]{2,1,0:T(8,128)} %get-tuple-element.147.refs_0_.refs_1_, ...), custom_call_target="tpu_custom_call", output_to_operand_aliasing={{4}: (11, {}), {5}: (12, {})} | custom-call | flops 22548578304 | bytes 38230016 | tf_op jit(solution)/shard_map/channel_1/pallas_call | solution.py:704
  159.3 46.9 %channel_2.1 = (bf16[2,512,768]{2,1,0:T(8,128)(2,1)}, f32[2,512,768]{2,1,0:T(8,128)}, f32[2,1,768]{2,1,0:T(1,128)}, f32[768,768]{1,0:T(8,128)}, f32[2,768]{1,0:T...) custom-call(f32[2,512,768]{2,1,0:T(8,128)} %get-tuple-element.147.re, ...), custom_call_target="tpu_custom_call", output_to_operand_aliasing={{7}: (13, {}), {8}: (14, {}), {9}: (15, {}), {10}: (16, {})} | custom-call | flops 22548578304 | bytes 40994816 | tf_op jit(solution)/shard_map/channel_2/pallas_call | solution.py:704
  206.2 40.8 %attention_back.1 = (f32[2,512,768]{2,1,0:T(8,128)}, f32[2,512,768]{2,1,0:T(8,128)}, f32[2,512,768]{2,1,0:T(8,128)}, f32[2,6,64,128]{3,2,1,0:T(8,128)}, f32[768,...) custom-call(f32[2,512,768]{2,1,0:T(8,128)} %get-tuple-element.163.re, ...), custom_call_target="tpu_custom_call", output_to_operand_aliasing={{6}: (10, {}), {7}: (11, {}), {8}: (12, {}), {9}: (13, {}),... | custom-call | flops 2415919104 | bytes 30771200 | tf_op jit(solution)/shard_map/attention_back/pallas_call | solution.py:704
  247.0 75.5 %mix_back.1 = (f32[2,512,768]{2,1,0:T(8,128)}, f32[2,512,768]{2,1,0:T(8,128)}, f32[2,512,768]{2,1,0:T(8,128)}, f32[2,2,768]{2,1,0:T(2,128)}, f32[2,6,64,128]{3,2...) custom-call(f32[2,512,768]{2,1,0:T(8,128)} %get-tuple-element.138.re, ...), custom_call_target="tpu_custom_call", output_to_operand_aliasing={{5}: (11, {}), {6}: (12, {}), {7}: (13, {}), {8}: (14, {}),... | custom-call | flops 14495514624 | bytes 22511616 | tf_op jit(solution)/shard_map/mix_back/pallas_call | solution.py:704
  322.5 50.7 %weights_back.1 = (f32[768,768]{1,0:T(8,128)}, f32[768,768]{1,0:T(8,128)}, f32[768,768]{1,0:T(8,128)}, f32[768,768]{1,0:T(8,128)}, f32[2,512,768]{2,1,0:T(8,128)...) custom-call(bf16[2,512,768]{2,1,0:T(8,128)(2,1)} %refs_0_.9, ...), custom_call_target="tpu_custom_call", output_to_operand_aliasing={{7}: (12, {}), {8}: (13, {}), {9}: (14, {}), {10}: (15, {})... | custom-call | flops 14495514624 | bytes 37053440 | tf_op jit(solution)/shard_map/weights_back/pallas_call | solution.py:704
  373.2 104.3 %inputs_back.1 = (f32[2,512,768]{2,1,0:T(8,128)}, f32[2,1,768]{2,1,0:T(1,128)}, f32[16,768]{1,0:T(8,128)}, f32[768,640]{1,0:T(8,128)}, f32[640,768]{1,0:T(8,128)...) custom-call(bf16[2,512,768]{2,1,0:T(8,128)(2,1)} %refs_0_.9, ...), custom_call_target="tpu_custom_call", output_to_operand_aliasing={{3}: (17, {}), {4}: (18, {}), {5}: (19, {}), {6}: (20, {}),... | custom-call | flops 9663676416 | bytes 25342976 | tf_op jit(solution)/shard_map/inputs_back/pallas_call | solution.py:704
  477.5 0.0 copy-start
  477.5 24.9 %gather.1 = (f32[768,2688]{1,0:T(8,128)}, f32[2688,768]{1,0:T(8,128)}, f32[768,768]{1,0:T(8,128)}, f32[768,768]{1,0:T(8,128)}, f32[768,768]{1,0:T(8,128)}, /*ind...) custom-call(f32[768,1024]{1,0:T(8,128)} %get-tuple-element.182.refs_, ...), custom_call_target="tpu_custom_call" | custom-call | bytes 67731456 | tf_op jit(solution)/shard_map/gather/pallas_call | solution.py:704
  502.4 0.0 copy-done
  502.4 1.1 copy.123
  (1 shorter events, 0.0 us)
Async XLA Ops:
  1.4 4.8 collective-permute-start
  477.5 24.9 %copy-start = (bf16[2,512,768]{2,1,0:T(8,128)(2,1)S(1)}, bf16[2,512,768]{2,1,0:T(8,128)(2,1)}, u32[]{:S(2)}) copy-start(bf16[2,512,768]{2,1,0:T(8,128)(2,1)} %get-tuple-element.270) | copy-start | bytes 4718596
